TPU v7x, 512 devices: a whole 4x8x8 slice. The times are simulated.
512 devices in a mesh: gx: 16 (over z, core), gy: 32 (over y, x).
Axes of the slice: x: 4, y: 8, z: 8, core: 2. Of those that a mesh axis runs over, the one named last changes fastest.
Arguments:
- source: float32 [128, 256, 512], P('gx', 'gy'), may hold values from -60 to 60
- conductivity: float32 [128, 256, 512], P('gx', 'gy'), may hold values from 0.5 to 5
- robin_flags: int32 [16, 32, 64], P('gx', 'gy'), may hold values from 0 to 63
- htc_class: int32 [16, 32, 64], P('gx', 'gy'), may hold values from 0 to 3
- htc_table: float32 [4], replicated, may hold values from 0.5 to 8
Outputs:
- adjoint: float32 [128, 256, 512], P('gx', 'gy')
- residual: float32 [128, 256, 512], P('gx', 'gy')
Inputs may be any that keep to these rules, and one draw needn't show every extreme that they name: `robin_flags`: bit f (value 2^f) flags face f of the element, in the order x-min, x-max, y-min, y-max, z-min, z-max.
All inputs are finite; a program needn't handle non-finite values.
Results may differ from a plain program's by a relative error of at most 0.0003.
Values sent between devices are 32-bit elements; how exact they have to be, the bound alone decides.
A program may use at most 64 MiB of HBM per device.

v0:
```python
import jax
import jax.numpy as jnp
import numpy as np
from jax import lax
from jax.sharding import PartitionSpec as P

ITERS = 3


gll_points = (
    -1.0,
    -0.8717401485096066,
    -0.5917001814331423,
    -0.2092992179024789,
    0.2092992179024789,
    0.5917001814331423,
    0.8717401485096066,
    1.0,
)
gll_weights = (
    0.03571428571428571,
    0.21070422714350603,
    0.3411226924835044,
    0.4124587946587038,
    0.4124587946587038,
    0.3411226924835044,
    0.21070422714350603,
    0.03571428571428571,
)
mass_coef = 0.2
scan_speed = 2.0
highest = lax.Precision.HIGHEST


def extended(block, sides, width):
    for axis, dim in sides:
        count = lax.axis_size(axis)
        forward = [(i, i + 1) for i in range(count - 1)]
        backward = [(target, source) for source, target in forward]
        low = lax.ppermute(
            lax.slice_in_dim(block, block.shape[dim] - width, None, axis=dim), axis, forward
        )
        high = lax.ppermute(lax.slice_in_dim(block, 0, width, axis=dim), axis, backward)
        block = jnp.concatenate([low, block, high], axis=dim)
    return block


def lagrange_derivative():
    points = np.array(gll_points)
    barycentric = np.array(
        [1.0 / np.prod([points[j] - points[m] for m in range(8) if m != j]) for j in range(8)]
    )
    derivative = np.zeros((8, 8))
    for a in range(8):
        for b in range(8):
            if a != b:
                derivative[a, b] = barycentric[b] / barycentric[a] / (points[a] - points[b])
        derivative[a, a] = -np.sum(derivative[a])
    return jnp.asarray(derivative, jnp.float32)


def edge_weights(elements):
    return jnp.tile(jnp.asarray(np.array(gll_weights), jnp.float32), elements)


def copies_along(elements, first_element, total_elements):
    node_index = jnp.arange(8 * elements) % 8
    element_index = first_element + jnp.arange(8 * elements) // 8
    shared = (node_index == 7) & (element_index < total_elements - 1) | (node_index == 0) & (
        element_index > 0
    )
    return jnp.where(shared, 2.0, 1.0).astype(jnp.float32)


def fold_inside(values, which_axis):
    moved_field = jnp.moveaxis(values, which_axis, 0)
    extent = moved_field.shape
    blocks = moved_field.reshape((extent[0] // 8, 8) + extent[1:])
    shared = blocks[:-1, 7] + blocks[1:, 0]
    blocks = blocks.at[:-1, 7].set(shared).at[1:, 0].set(shared)
    return jnp.moveaxis(blocks.reshape(extent), 0, which_axis)


def element_expand(elements):
    return (jnp.arange(8 * elements)[None, :] // 8 == jnp.arange(elements)[:, None]).astype(
        jnp.float32
    )


def robin_field(robin_flags, htc_class, htc_table, start_x, start_y, total_x, total_y):
    elems_x, elems_y, elems_z = robin_flags.shape
    class_hits = (htc_class[..., None] == jnp.arange(htc_table.shape[0])).astype(jnp.float32)
    coefficient = jnp.sum(class_hits * htc_table, axis=-1)
    index_x = (start_x + jnp.arange(elems_x))[:, None, None]
    index_y = (start_y + jnp.arange(elems_y))[None, :, None]
    index_z = jnp.arange(elems_z)[None, None, :]
    boundary = [
        index_x == 0,
        index_x == total_x - 1,
        index_y == 0,
        index_y == total_y - 1,
        index_z == 0,
        index_z == elems_z - 1,
    ]
    weight_x = edge_weights(elems_x)
    weight_y = edge_weights(elems_y)
    weight_z = edge_weights(elems_z)
    node_x = (jnp.arange(8 * elems_x) % 8)[:, None, None]
    node_y = (jnp.arange(8 * elems_y) % 8)[None, :, None]
    node_z = (jnp.arange(8 * elems_z) % 8)[None, None, :]
    cross_x = weight_y[None, :, None] * weight_z[None, None, :]
    cross_y = weight_x[:, None, None] * weight_z[None, None, :]
    cross_z = weight_x[:, None, None] * weight_y[None, :, None]
    patterns = [
        (node_x == 0) * cross_x,
        (node_x == 7) * cross_x,
        (node_y == 0) * cross_y,
        (node_y == 7) * cross_y,
        (node_z == 0) * cross_z,
        (node_z == 7) * cross_z,
    ]
    expand_x = element_expand(elems_x)
    expand_y = element_expand(elems_y)
    expand_z = element_expand(elems_z)
    robin_sum = jnp.zeros((8 * elems_x, 8 * elems_y, 8 * elems_z), jnp.float32)
    for face_bit in range(6):
        flag_bit = (robin_flags // (1 << face_bit) % 2).astype(jnp.float32)
        coef_face = (
            coefficient
            * flag_bit
            * jnp.broadcast_to(boundary[face_bit], robin_flags.shape).astype(jnp.float32)
        )
        spread = jnp.einsum("ai,bj,abc->ijc", expand_x, expand_y, coef_face, precision=highest)
        spread = jnp.einsum("ijc,ck->ijk", spread, expand_z, precision=highest)
        robin_sum = robin_sum + spread * patterns[face_bit]
    return robin_sum


def per_device(source, conductivity, robin_flags, htc_class, htc_table):
    elems_x, elems_y, elems_z = robin_flags.shape
    start_x = lax.axis_index("gx") * elems_x
    start_y = lax.axis_index("gy") * elems_y
    total_x = elems_x * lax.axis_size("gx")
    total_y = elems_y * lax.axis_size("gy")
    derivative = lagrange_derivative()
    deriv_x = jnp.kron(jnp.eye(elems_x, dtype=jnp.float32), derivative)
    deriv_y = jnp.kron(jnp.eye(elems_y, dtype=jnp.float32), derivative)
    tile_z = 8 * min(elems_z, 16)
    deriv_z = jnp.kron(jnp.eye(tile_z // 8, dtype=jnp.float32), derivative)
    weight_x = edge_weights(elems_x)
    weight_y = edge_weights(elems_y)
    weight_z = edge_weights(elems_z)
    weights = weight_x[:, None, None] * weight_y[None, :, None] * weight_z[None, None, :]
    copies_x = copies_along(elems_x, start_x, total_x)
    copies_y = copies_along(elems_y, start_y, total_y)
    copies_z = copies_along(elems_z, 0, elems_z)
    inv_copies = 1.0 / (copies_x[:, None, None] * copies_y[None, :, None] * copies_z[None, None, :])
    robin_diag = robin_field(robin_flags, htc_class, htc_table, start_x, start_y, total_x, total_y)
    rows_x, rows_y, rows_z = source.shape
    tiled_shape = (rows_x, rows_y, rows_z // tile_z, tile_z)

    def assemble(values):
        local_sum = fold_inside(fold_inside(fold_inside(values, 0), 1), 2)
        padded = extended(local_sum, (("gx", 0), ("gy", 1)), 1)
        inner_rows = padded[1:-1].at[0].add(padded[0]).at[-1].add(padded[-1])
        return inner_rows[:, 1:-1].at[:, 0].add(inner_rows[:, 0]).at[:, -1].add(inner_rows[:, -1])

    def operate(values):
        grad_x = jnp.einsum("ij,jbc->ibc", deriv_x, values, precision=highest)
        grad_y = jnp.einsum("ij,ajc->aic", deriv_y, values, precision=highest)
        grad_z = jnp.einsum(
            "abkj,ij->abki", values.reshape(tiled_shape), deriv_z, precision=highest
        ).reshape(source.shape)
        flux_x = weights * (conductivity * grad_x - scan_speed * values)
        flux_y = weights * conductivity * grad_y
        flux_z = weights * conductivity * grad_z
        back_x = jnp.einsum("ij,ibc->jbc", deriv_x, flux_x, precision=highest)
        back_y = jnp.einsum("ij,aic->ajc", deriv_y, flux_y, precision=highest)
        back_z = jnp.einsum(
            "abki,ij->abkj", flux_z.reshape(tiled_shape), deriv_z, precision=highest
        ).reshape(source.shape)
        local_terms = mass_coef * weights * values + robin_diag * values + back_x + back_y + back_z
        return assemble(local_terms)

    def local_inner(left, right):
        return jnp.sum(left * right * inv_copies)

    assembled = assemble(weights * source)
    adjoint = jnp.zeros_like(assembled)
    residual = assembled
    direction = assembled
    rho_now = lax.psum(local_inner(assembled, assembled), ("gx", "gy"))
    for iteration in range(ITERS):
        applied = operate(direction)
        alpha_step = rho_now / lax.psum(local_inner(assembled, applied), ("gx", "gy"))
        half_resid = residual - alpha_step * applied
        applied_half = operate(half_resid)
        cross_sum, square_sum = lax.psum(
            (local_inner(applied_half, half_resid), local_inner(applied_half, applied_half)),
            ("gx", "gy"),
        )
        omega_step = cross_sum / square_sum
        adjoint = adjoint + alpha_step * direction + omega_step * half_resid
        residual = half_resid - omega_step * applied_half
        if iteration + 1 < ITERS:
            rho_next = lax.psum(local_inner(assembled, residual), ("gx", "gy"))
            beta_step = rho_next / rho_now * (alpha_step / omega_step)
            direction = residual + beta_step * (direction - omega_step * applied)
            rho_now = rho_next
    return (adjoint, residual)


def solution(mesh):
    return jax.shard_map(
        per_device,
        mesh=mesh,
        in_specs=(
            P("gx", "gy", None),
            P("gx", "gy", None),
            P("gx", "gy", None),
            P("gx", "gy", None),
            P(),
        ),
        out_specs=(P("gx", "gy", None), P("gx", "gy", None)),
        check_vma=False,
    )
```

profile of v0, /device:TPU:1, one launch (start us, length us, event | category | flops | bytes accessed | tf_op | source)
XLA Modules:
  0.0 1214.8 jit_solution(14653062821189367658)
XLA Ops:
  5.7 5.0 dynamic-slice_select_fusion.6
  10.7 17.8 %scatter.46 = f32[64,8,8,8]{1,0,3,2:T(8,128)S(1)} dynamic-update-slice(f32[64,8,8,8]{1,0,3,2:T(8,128)S(1)} %reshape.1990, f32[63,1,8,8]{1,0,3,2:T(8,128)} %get-tuple-element.536, s32[]{:T(128)} %bitcast.1, s32[]{:T(128)} %bitcast.2, s32[]{:T(128)} %constant.1114.clone.1, s32[]{:T(128)} %constant.1114.clone.1) | dynamic-update-slice | bytes 32260 | tf_op jit(solution)/shard_map/scatter | solution.py:80
  28.5 10.4 scatter.49
  40.1 5.4 collective-permute-start
  45.5 4.7 collective-permute-start.1
  55.5 2.8 collective-permute-done.3
  62.4 5.0 dynamic-slice_select_fusion.5
  67.4 17.8 %scatter.50 = f32[64,8,8,8]{1,0,3,2:T(8,128)S(1)} dynamic-update-slice(f32[64,8,8,8]{1,0,3,2:T(8,128)S(1)} %reshape.2005, f32[63,1,8,8]{1,0,3,2:T(8,128)} %get-tuple-element.534, s32[]{:T(128)} %bitcast.1, s32[]{:T(128)} %bitcast.2, s32[]{:T(128)} %constant.1114.clone.1, s32[]{:T(128)} %constant.1114.clone.1) | dynamic-update-slice | bytes 32260 | tf_op jit(solution)/shard_map/scatter | solution.py:80
  85.2 10.4 scatter.51
  96.8 4.0 collective-permute-start.4
  102.8 3.1 collective-permute-done.5
  105.9 3.1 collective-permute-start.6
  110.3 3.2 collective-permute-done.7
  114.8 109.6 %all-reduce.3 = (f32[]{:T(128)}, f32[]{:T(128)}) all-reduce(f32[]{:T(128)} %get-tuple-element.513, f32[]{:T(128)} %get-tuple-element.512), channel_id=1, replica_groups=mesh['gx'=16,'gy'=32] {'gx','gy'}, use_global_device_ids=true, to_apply=%region_2.3 | all-reduce | flops 2 | bytes 16 | tf_op jit(solution)/shard_map/psum | solution.py:192
  228.8 5.0 dynamic-slice_select_fusion.4
  233.8 17.8 %scatter.54 = f32[64,8,8,8]{1,0,3,2:T(8,128)S(1)} dynamic-update-slice(f32[64,8,8,8]{1,0,3,2:T(8,128)S(1)} %reshape.2011, f32[63,1,8,8]{1,0,3,2:T(8,128)} %get-tuple-element.532, s32[]{:T(128)} %bitcast.1, s32[]{:T(128)} %bitcast.2, s32[]{:T(128)} %constant.1114.clone.1, s32[]{:T(128)} %constant.1114.clone.1) | dynamic-update-slice | bytes 32260 | tf_op jit(solution)/shard_map/scatter | solution.py:80
  251.6 10.4 scatter.55
  267.5 2.9 collective-permute-done.9
  273.7 3.2 collective-permute-done.11
  278.1 104.4 %all-reduce.2 = (f32[]{:T(128)}, f32[]{:T(128)}) all-reduce(f32[]{:T(128)} %get-tuple-element.511, f32[]{:T(128)} %get-tuple-element.510), channel_id=1, replica_groups=mesh['gx'=16,'gy'=32] {'gx','gy'}, use_global_device_ids=true, to_apply=%region_7.8 | all-reduce | flops 2 | bytes 16 | tf_op jit(solution)/shard_map/psum | solution.py:198
  387.0 95.1 %psum.88 = f32[]{:T(128)} all-reduce(f32[]{:T(128)} %multiply_reduce_fusion.7), channel_id=1, replica_groups=mesh['gx'=16,'gy'=32] {'gx','gy'}, use_global_device_ids=true, to_apply=%region_11.12 | all-reduce | flops 1 | bytes 8 | tf_op jit(solution)/shard_map/psum | solution.py:206
  486.6 5.0 dynamic-slice_select_fusion.3
  491.6 17.8 %scatter.56 = f32[64,8,8,8]{1,0,3,2:T(8,128)S(1)} dynamic-update-slice(f32[64,8,8,8]{1,0,3,2:T(8,128)S(1)} %reshape.2017, f32[63,1,8,8]{1,0,3,2:T(8,128)} %get-tuple-element.530, s32[]{:T(128)} %bitcast.1, s32[]{:T(128)} %bitcast.2, s32[]{:T(128)} %constant.1114.clone.1, s32[]{:T(128)} %constant.1114.clone.1) | dynamic-update-slice | bytes 32260 | tf_op jit(solution)/shard_map/scatter | solution.py:80
  509.4 10.4 scatter.59
  525.6 3.1 collective-permute-done.13
  528.7 3.7 collective-permute-start.14
  533.7 3.2 collective-permute-done.15
  538.1 101.1 %psum.89 = f32[]{:T(128)} all-reduce(f32[]{:T(128)} %multiply_reduce_fusion.6), channel_id=1, replica_groups=mesh['gx'=16,'gy'=32] {'gx','gy'}, use_global_device_ids=true, to_apply=%region_13.14 | all-reduce | flops 1 | bytes 8 | tf_op jit(solution)/shard_map/psum | solution.py:195
  643.5 5.0 dynamic-slice_select_fusion.2
  648.5 17.8 %scatter.60 = f32[64,8,8,8]{1,0,3,2:T(8,128)S(1)} dynamic-update-slice(f32[64,8,8,8]{1,0,3,2:T(8,128)S(1)} %reshape.2023, f32[63,1,8,8]{1,0,3,2:T(8,128)} %get-tuple-element.528, s32[]{:T(128)} %bitcast.1, s32[]{:T(128)} %bitcast.2, s32[]{:T(128)} %constant.1114.clone.1, s32[]{:T(128)} %constant.1114.clone.1) | dynamic-update-slice | bytes 32260 | tf_op jit(solution)/shard_map/scatter | solution.py:80
  666.4 10.4 scatter.61
  682.4 3.1 collective-permute-done.17
  688.6 3.2 collective-permute-done.19
  693.1 104.4 %all-reduce.1 = (f32[]{:T(128)}, f32[]{:T(128)}) all-reduce(f32[]{:T(128)} %get-tuple-element.509, f32[]{:T(128)} %get-tuple-element.508), channel_id=1, replica_groups=mesh['gx'=16,'gy'=32] {'gx','gy'}, use_global_device_ids=true, to_apply=%region_15.16 | all-reduce | flops 2 | bytes 16 | tf_op jit(solution)/shard_map/psum | solution.py:198
  802.0 95.4 %psum.92 = f32[]{:T(128)} all-reduce(f32[]{:T(128)} %get-tuple-element.526), channel_id=1, replica_groups=mesh['gx'=16,'gy'=32] {'gx','gy'}, use_global_device_ids=true, to_apply=%region_19.20 | all-reduce | flops 1 | bytes 8 | tf_op jit(solution)/shard_map/psum | solution.py:206
  901.8 5.0 dynamic-slice_select_fusion.1
  906.8 17.8 %scatter.64 = f32[64,8,8,8]{1,0,3,2:T(8,128)S(1)} dynamic-update-slice(f32[64,8,8,8]{1,0,3,2:T(8,128)S(1)} %reshape.2029, f32[63,1,8,8]{1,0,3,2:T(8,128)} %get-tuple-element.524, s32[]{:T(128)} %bitcast.1, s32[]{:T(128)} %bitcast.2, s32[]{:T(128)} %constant.1114.clone.1, s32[]{:T(128)} %constant.1114.clone.1) | dynamic-update-slice | bytes 32260 | tf_op jit(solution)/shard_map/scatter | solution.py:80
  924.7 10.4 scatter.65
  940.8 3.1 collective-permute-done.21
  943.9 3.7 collective-permute-start.22
  948.9 3.2 collective-permute-done.23
  953.3 101.0 %psum.93 = f32[]{:T(128)} all-reduce(f32[]{:T(128)} %multiply_reduce_fusion.2), channel_id=1, replica_groups=mesh['gx'=16,'gy'=32] {'gx','gy'}, use_global_device_ids=true, to_apply=%region_21.22 | all-reduce | flops 1 | bytes 8 | tf_op jit(solution)/shard_map/psum | solution.py:195
  1058.6 5.0 dynamic-slice_select_fusion
  1063.6 17.8 %scatter.66 = f32[64,8,8,8]{1,0,3,2:T(8,128)S(1)} dynamic-update-slice(f32[64,8,8,8]{1,0,3,2:T(8,128)S(1)} %reshape.2035, f32[63,1,8,8]{1,0,3,2:T(8,128)} %get-tuple-element.522, s32[]{:T(128)} %bitcast.1, s32[]{:T(128)} %bitcast.2, s32[]{:T(128)} %constant.1114.clone.1, s32[]{:T(128)} %constant.1114.clone.1) | dynamic-update-slice | bytes 32260 | tf_op jit(solution)/shard_map/scatter | solution.py:80
  1081.4 10.4 scatter.69
  1097.4 3.1 collective-permute-done.25
  1103.7 3.2 collective-permute-done.27
  1108.1 104.4 %all-reduce = (f32[]{:T(128)}, f32[]{:T(128)}) all-reduce(f32[]{:T(128)} %get-tuple-element.507, f32[]{:T(128)} %get-tuple-element.506), channel_id=1, replica_groups=mesh['gx'=16,'gy'=32] {'gx','gy'}, use_global_device_ids=true, to_apply=%region_23.24 | all-reduce | flops 2 | bytes 16 | tf_op jit(solution)/shard_map/psum | solution.py:198
  (228 shorter events, 84.3 us)
Async XLA Ops:
  0.6 4.3 copy-start.5
  38.9 11.4 copy-start.2
  38.9 11.5 copy-start.6
  38.9 11.5 copy-start.7
  38.9 11.6 copy-start.4
  38.9 12.7 %copy-start.3 = (f32[8,8]{1,0:T(8,128)S(1)}, f32[8,8]{1,0:T(8,128)}, u32[]{:S(2)}) copy-start(f32[8,8]{1,0:T(8,128)} %constant.1136.clone) | copy-start | bytes 772
  40.1 12.2 %collective-permute-start = (f32[1,8,512]{2,1,0:T(8,128)S(1)}, f32[1,8,512]{2,1,0:T(8,128)S(1)}, u32[]{:S(2)}, u32[]{:S(2)}) collective-permute-start(f32[1,8,512]{2,1,0:T(8,128)S(1)} %get-tuple-element.566), channel_id=1, source_target_pairs={{0,32},{32,64},{64,96},{96,128},{128,160},{160,192},{192,224},{224... | collective-permute-start | bytes 49160 | tf_op jit(solution)/shard_map/ppermute | solution.py:40
  45.5 6.8 collective-permute-start.1
  51.7 7.6 copy-start.1
  51.8 7.9 copy-start
  52.4 3.2 collective-permute-start.2
  53.7 4.6 collective-permute-start.3
  96.8 6.0 collective-permute-start.4
  100.8 5.1 collective-permute-start.5
  105.9 4.4 collective-permute-start.6
  109.0 4.5 collective-permute-start.7
  263.2 4.3 collective-permute-start.8
  265.4 5.1 collective-permute-start.9
  270.5 3.2 collective-permute-start.10
  272.3 4.5 collective-permute-start.11
  521.0 4.6 collective-permute-start.12
  523.7 5.1 collective-permute-start.13
  528.7 5.0 collective-permute-start.14
  532.4 4.5 collective-permute-start.15
  677.9 4.4 collective-permute-start.16
  680.4 5.1 collective-permute-start.17
  685.5 3.1 collective-permute-start.18
  687.3 4.5 collective-permute-start.19
  936.2 4.6 collective-permute-start.20
  938.9 5.1 collective-permute-start.21
  943.9 5.0 collective-permute-start.22
  947.6 4.5 collective-permute-start.23
  1093.0 4.4 collective-permute-start.24
  1095.5 5.1 collective-permute-start.25
  1100.6 3.1 collective-permute-start.26
  1102.4 4.5 collective-permute-start.27
where the time goes:
time: 1220 us; the launch traced here: 1210 us
  blocking collectives  816 us (67%)
  local copies, waits for them, and re-layouts  218 us (18%)
  starting transfers between devices  64.5 us (5%)
  other arithmetic  46.8 us (4%)
  waiting for transfers between devices  40.5 us (3%)
  between operations  17.7 us (1%)
    psum x3, blocking collectives, per_device(): lax.psum((local_inner(applied_half, half_resid), local_inner(applied_half...  313 us
    psum x2, blocking collectives, per_device(): lax.psum(local_inner(assembled, applied), ('gx', 'gy'))  202 us
    scatter x14, local copies, waits for them, and re-layouts, fold_inside(): blocks = blocks.at[:-1, 7].set(shared).at[1:, 0].set(shared)  197 us
    psum x2, blocking collectives, per_device(): rho_next = lax.psum(local_inner(assembled, residual), ('gx', 'gy'))  191 us
    psum x1, blocking collectives, per_device(): rho_now = lax.psum(local_inner(assembled, assembled), ('gx', 'gy'))  110 us
    ppermute x14, waiting for transfers between devices, extended(): lax.ppermute(lax.slice_in_dim(block, 0, width, axis=dim), axis, backward)  40.5 us
    ppermute x14, starting transfers between devices, extended(): lax.ppermute(lax.slice_in_dim(block, block.shape[dim] - width, None, axis...  39.1 us
    another operation x11, other arithmetic  35.8 us
  transfers between devices with their start and end apart: 28, of which 13 were waited for; matrix products, arithmetic and copies ran while one was open for 0% of the time, Pallas kernels for 0%

commit v1 on v0

v1 whole, which is shorter than its diff:
```python
import functools

import jax
import jax.numpy as jnp
import numpy as np
from jax import lax
from jax.experimental import pallas as pl
from jax.experimental.pallas import tpu as pltpu
from jax.sharding import PartitionSpec as P

MESH = pl.DeviceIdType.MESH
HIGHEST = lax.Precision.HIGHEST
f32 = jnp.float32

gll_points = (
    -1.0,
    -0.8717401485096066,
    -0.5917001814331423,
    -0.2092992179024789,
    0.2092992179024789,
    0.5917001814331423,
    0.8717401485096066,
    1.0,
)
gll_weights = (
    0.03571428571428571,
    0.21070422714350603,
    0.3411226924835044,
    0.4124587946587038,
    0.4124587946587038,
    0.3411226924835044,
    0.21070422714350603,
    0.03571428571428571,
)
mass_coef = 0.2
scan_speed = 2.0
ROUNDS = 7
SUMS = 3


def derivative_matrix():
    points = np.array(gll_points)
    bary = np.array(
        [1.0 / np.prod([points[j] - points[m] for m in range(8) if m != j]) for j in range(8)]
    )
    d = np.zeros((8, 8))
    for a in range(8):
        for b in range(8):
            if a != b:
                d[a, b] = bary[b] / bary[a] / (points[a] - points[b])
        d[a, a] = -np.sum(d[a])
    return d


D = derivative_matrix()


def along_planes(planes, mat):
    even = [planes[b] + planes[7 - b] for b in range(4)]
    odd = [planes[b] - planes[7 - b] for b in range(4)]
    out = [None] * 8
    for a in range(4):
        p = sum(float(0.5 * (mat[a, b] + mat[a, 7 - b])) * even[b] for b in range(4))
        q = sum(float(0.5 * (mat[a, b] - mat[a, 7 - b])) * odd[b] for b in range(4))
        out[a] = p + q
        out[7 - a] = q - p
    return out


def kernel(
    nx, ny, nz,
    src_hbm, cond_hbm, flags_hbm, class_hbm, table_ref, mats_hbm, kmat_hbm, planes_hbm,
    adj_ref, res_ref,
    src, wk, flags, classes, mats, kmat, planes, mass, im,
    loc, vec, xr, yr, cr, ysend, csend,
    parts, msg1, msg2, buf1, buf2,
    in_sem, send_x, send_y, send_c, recv_x, recv_y, recv_c,
    send_1, send_2, recv_1, recv_2,
):
    gx = lax.axis_index("gx")
    gy = lax.axis_index("gy")

    def at_x(k):
        return lax.rem(gx + (k % nx), nx)

    def at_y(k):
        return lax.rem(gy + (k % ny), ny)

    loads = [
        pltpu.make_async_copy(a, b, in_sem.at[i])
        for i, (a, b) in enumerate(
            [
                (planes_hbm, planes),
                (src_hbm, src),
                (cond_hbm, wk),
                (flags_hbm, flags),
                (class_hbm, classes),
                (mats_hbm, mats),
                (kmat_hbm, kmat),
            ]
        )
    ]
    for c in loads:
        c.start()

    barrier = pltpu.get_barrier_semaphore()
    order_x = sorted(range(1, nx), key=lambda k: abs(k - nx // 2))
    order_y = sorted(range(1, ny), key=lambda k: abs(k - ny // 2))
    peers = [(at_x(dx), at_y(dy)) for dx in (-1, 1) for dy in (-1, 1)]
    peers += [(gx, at_y(k)) for k in order_y] + [(at_x(k), gy) for k in order_x]
    for peer in peers:
        pl.semaphore_signal(barrier, inc=1, device_id=peer, device_id_type=MESH)

    lane = lax.broadcasted_iota(jnp.int32, (8, nz), 1)
    node_z = lax.rem(lane, 8)
    row = lax.broadcasted_iota(jnp.int32, (8, nz), 0)
    join_up = (node_z == 7) & (lane < nz - 1)
    join_dn = (node_z == 0) & (lane > 0)
    zero = jnp.zeros((8, nz), f32)
    x_lo, x_hi = gx > 0, gx < nx - 1
    y_lo, y_hi = gy > 0, gy < ny - 1

    def zfold(plane):
        up = pltpu.roll(plane, nz - 1, 1)
        dn = pltpu.roll(plane, 1, 1)
        return plane + jnp.where(join_up, up, jnp.where(join_dn, dn, zero))

    for c in loads[:2]:
        c.wait()
    w_yz = planes[0]
    inv_z = planes[1]

    def put_local(k, x, plane):
        loc[k, x] = plane
        ysend[k, 0, pl.ds(x, 1), :] = plane[0:1]
        ysend[k, 1, pl.ds(x, 1), :] = plane[7:8]
        if x in (0, 7):
            csend[k, 0 if x == 0 else 2] = plane[0:1]
            csend[k, 1 if x == 0 else 3] = plane[7:8]

    def halo_start(k):
        def send(s, d, ss, rs, peer):
            pltpu.make_async_remote_copy(
                src_ref=s, dst_ref=d, send_sem=ss, recv_sem=rs,
                device_id=peer, device_id_type=MESH,
            ).start()

        for i, (dx, dy) in enumerate(((-1, -1), (-1, 1), (1, -1), (1, 1))):
            send(csend.at[k, i], cr.at[k, 3 - i], send_c, recv_c.at[k], (at_x(dx), at_y(dy)))
        for i, dy in enumerate((-1, 1)):
            send(ysend.at[k, i], yr.at[k, 1 - i], send_y, recv_y.at[k], (gx, at_y(dy)))
        for i, dx in enumerate((-1, 1)):
            send(loc.at[k, 7 * i], xr.at[k, 1 - i], send_x, recv_x.at[k], (at_x(dx), gy))

    def halo_wait(k):
        pltpu.make_async_copy(xr.at[k], xr.at[k], recv_x.at[k]).wait()
        pltpu.make_async_copy(yr.at[k], yr.at[k], recv_y.at[k]).wait()
        pltpu.make_async_copy(cr.at[k], cr.at[k], recv_c.at[k]).wait()

    def assembled_plane(k, x):
        plane = loc[k, x]
        lo = jnp.broadcast_to(yr[k, 0, pl.ds(x, 1), :], (8, nz))
        hi = jnp.broadcast_to(yr[k, 1, pl.ds(x, 1), :], (8, nz))
        if x in (0, 7):
            i = 0 if x == 0 else 1
            has = x_lo if x == 0 else x_hi
            lo = lo + jnp.where(has, jnp.broadcast_to(cr[k, 2 * i], (8, nz)), zero)
            hi = hi + jnp.where(has, jnp.broadcast_to(cr[k, 2 * i + 1], (8, nz)), zero)
            plane = plane + jnp.where(has, xr[k, i], zero)
        add = jnp.where((row == 0) & y_lo, lo, jnp.where((row == 7) & y_hi, hi, zero))
        return plane + add

    def halo_finish(k, dst):
        halo_wait(k)
        for x in range(8):
            vec[dst, x] = assembled_plane(k, x)

    for x in range(8):
        put_local(0, x, zfold(float(gll_weights[x]) * w_yz * src[x]))

    for c in loads[2:]:
        c.wait()
    bits = flags[...]
    kinds = classes[...]
    coef = jnp.zeros(kinds.shape, f32)
    for i in range(4):
        coef = coef + jnp.where(kinds == i, table_ref[i], 0.0)

    pl.semaphore_wait(barrier, len(peers))
    halo_start(0)

    edge = [gx == 0, gx == nx - 1, gy == 0, gy == ny - 1]
    faces = []
    for i in range(6):
        bit = lax.bitwise_and(lax.shift_right_logical(bits, i), 1).astype(f32)
        face = coef * bit
        if i < 4:
            face = jnp.where(edge[i], face, 0.0)
        faces.append(face)
    faces = jnp.concatenate(faces + [jnp.zeros((2, kinds.shape[1]), f32)], axis=0)
    elem = lax.broadcasted_iota(jnp.int32, (kinds.shape[1], nz), 0)
    spread = (lax.broadcasted_iota(jnp.int32, (kinds.shape[1], nz), 1) // 8 == elem).astype(f32)
    wide = jnp.dot(faces, spread, precision=HIGHEST, preferred_element_type=f32)

    def line(i):
        return jnp.broadcast_to(wide[i : i + 1], (8, nz))

    w_y = planes[2]
    w_z = planes[3]
    side_y = jnp.where(row == 0, line(2), jnp.where(row == 7, line(3), zero)) * w_z
    side_z = jnp.where(lane == 0, line(4), jnp.where(lane == nz - 1, line(5), zero)) * w_y
    inv_y = jnp.where(((row == 0) & y_lo) | ((row == 7) & y_hi), 0.5, 1.0).astype(f32)
    inv_yz = inv_y * inv_z
    for x in range(8):
        wx = float(gll_weights[x])
        robin = wx * (side_y + side_z)
        inv = inv_yz
        if x == 0:
            robin = robin + line(0) * w_yz
            inv = jnp.where(x_lo, 0.5 * inv_yz, inv_yz)
        if x == 7:
            robin = robin + line(1) * w_yz
            inv = jnp.where(x_hi, 0.5 * inv_yz, inv_yz)
        mass[x] = (mass_coef * wx) * w_yz + robin
        im[x] = inv
        wk[x] = (wx * w_yz) * wk[x]

    chunks = [slice(128 * t, 128 * t + 128) for t in range(nz // 128)]

    def apply_local(s, k):
        v = [vec[s, x] for x in range(8)]
        grad_x = along_planes(v, D)
        flux_x = [
            wk[x] * grad_x[x] - (scan_speed * float(gll_weights[x])) * (w_yz * v[x])
            for x in range(8)
        ]
        back_x = along_planes(flux_x, D.T)
        acc = [mass[x] * v[x] + back_x[x] for x in range(8)]
        whole = vec[s].reshape(64, nz)
        wk2 = wk[...].reshape(64, nz)
        grad_y = jnp.dot(kmat[0], whole, precision=HIGHEST, preferred_element_type=f32)
        back = jnp.dot(kmat[1], wk2 * grad_y, precision=HIGHEST, preferred_element_type=f32)
        tall = jnp.concatenate([whole[:, c] for c in chunks], axis=0)
        wk_t = jnp.concatenate([wk2[:, c] for c in chunks], axis=0)
        grad_z = jnp.dot(tall, mats[0], precision=HIGHEST, preferred_element_type=f32)
        back_z = jnp.dot(wk_t * grad_z, mats[1], precision=HIGHEST, preferred_element_type=f32)
        back_z = jnp.concatenate(
            [back_z[64 * t : 64 * t + 64] for t in range(len(chunks))], axis=1
        )
        back = (back + back_z).reshape(8, 8, nz)
        for x in range(8):
            put_local(k, x, zfold(acc[x] + back[x]))

    parts[...] = jnp.zeros(parts.shape, f32)
    ones = jnp.ones((8, 128), f32)

    def put_dot(j, d, left, right):
        total = sum(left[x] * right[x] for x in range(8))
        parts[j, 8 * d : 8 * d + 8, :] = sum(total[:, c] for c in chunks)

    def planes_of(s):
        return [vec[s, x] for x in range(8)]

    def weighted(v):
        return [im[x] * v[x] for x in range(8)]

    def sum_start(j):
        rows = lax.dot_general(
            ones, parts[j], (((1,), (1,)), ((), ())),
            precision=HIGHEST, preferred_element_type=f32,
        )
        msg1[j] = rows[0:1]
        buf1[j, pl.ds(gx, 1)] = rows[0:1].reshape(1, 1, 128)
        for k in order_x:
            pltpu.make_async_remote_copy(
                src_ref=msg1.at[j], dst_ref=buf1.at[j, gx], send_sem=send_1,
                recv_sem=recv_1.at[j], device_id=(at_x(k), gy), device_id_type=MESH,
            ).start()

    def sum_middle(j):
        pltpu.make_async_copy(
            buf1.at[j, pl.ds(0, nx - 1)], buf1.at[j, pl.ds(0, nx - 1)], recv_1.at[j]
        ).wait()
        total = jnp.sum(buf1[j], axis=0)
        msg2[j] = total
        buf2[j, pl.ds(gy, 1)] = total.reshape(1, 1, 128)
        for k in order_y:
            pltpu.make_async_remote_copy(
                src_ref=msg2.at[j], dst_ref=buf2.at[j, gy], send_sem=send_2,
                recv_sem=recv_2.at[j], device_id=(gx, at_y(k)), device_id_type=MESH,
            ).start()

    pick = (
        lax.broadcasted_iota(jnp.int32, (16, 128), 1) // 8
        == lax.broadcasted_iota(jnp.int32, (16, 128), 0)
    )

    def sum_finish(j):
        pltpu.make_async_copy(
            buf2.at[j, pl.ds(0, ny - 1)], buf2.at[j, pl.ds(0, ny - 1)], recv_2.at[j]
        ).wait()
        total = jnp.broadcast_to(jnp.sum(buf2[j], axis=0), (16, 128))
        spread_rows = jnp.where(pick, total, 0.0)
        return jnp.dot(
            spread_rows, jnp.ones((128, 128), f32), precision=HIGHEST,
            preferred_element_type=f32,
        )

    def wide_of(scalar):
        return jnp.broadcast_to(jnp.concatenate([scalar] * len(chunks), axis=1), (8, nz))

    B, V1, V2, V3, V4, R, RA, RA2, RA3, PP, PA, PA2, PA3, PA4, X = range(15)

    halo_finish(0, B)
    apply_local(B, 1)
    halo_start(1)
    b = planes_of(B)
    bw = weighted(b)
    put_dot(0, 0, bw, b)
    halo_finish(1, V1)
    apply_local(V1, 2)
    halo_start(2)
    v1 = planes_of(V1)
    put_dot(0, 1, weighted(planes_of(B)), v1)
    put_dot(0, 2, weighted(v1), v1)
    halo_finish(2, V2)
    v2 = planes_of(V2)
    v2w = weighted(v2)
    put_dot(0, 3, v2w, planes_of(B))
    put_dot(0, 4, v2w, planes_of(V1))
    put_dot(0, 5, v2w, v2)
    sum_start(0)
    apply_local(V2, 3)
    halo_start(3)
    sum_middle(0)
    halo_finish(3, V3)
    apply_local(V3, 4)
    halo_start(4)
    halo_finish(4, V4)

    s = sum_finish(0)
    bb, bv1, v1v1, bv2, v1v2, v2v2 = [s[i : i + 1] for i in range(6)]
    rho = bb
    alpha = rho / bv1
    cross = bv1 - alpha * (v1v1 + bv2) + alpha * alpha * v1v2
    square = v1v1 - 2.0 * alpha * v1v2 + alpha * alpha * v2v2
    omega = cross / square
    rho_next = -omega * (bv1 - alpha * bv2)
    beta = rho_next / rho * (alpha / omega)
    rho = rho_next
    al, om, be = wide_of(alpha), wide_of(omega), wide_of(beta)
    for x in range(8):
        b, v1, v2, v3, v4 = [vec[i, x] for i in (B, V1, V2, V3, V4)]
        s0 = b - al * v1
        s1 = v1 - al * v2
        s2 = v2 - al * v3
        s3 = v3 - al * v4
        vec[X, x] = al * b + om * s0
        r0 = s0 - om * s1
        r1 = s1 - om * s2
        r2 = s2 - om * s3
        vec[R, x] = r0
        vec[RA, x] = r1
        vec[RA2, x] = r2
        vec[PP, x] = r0 + be * (b - om * v1)
        vec[PA, x] = r1 + be * (v1 - om * v2)
        vec[PA2, x] = r2 + be * (v2 - om * v3)

    def put_dots(j):
        ra = planes_of(RA)
        raw = weighted(ra)
        put_dot(j, 0, raw, planes_of(R))
        put_dot(j, 1, raw, planes_of(PA))
        put_dot(j, 2, raw, ra)
        pa2 = planes_of(PA2)
        pa2w = weighted(pa2)
        put_dot(j, 3, pa2w, planes_of(R))
        put_dot(j, 4, pa2w, planes_of(PA))
        put_dot(j, 5, pa2w, ra)
        put_dot(j, 6, pa2w, pa2)
        bw = weighted(planes_of(B))
        put_dot(j, 7, bw, planes_of(PA))
        if j == 1:
            put_dot(j, 8, bw, ra)
            put_dot(j, 9, bw, pa2)

    def steps(j, rho):
        s = sum_finish(j)
        (ra_r, ra_pa, ra_ra, p2_r, p2_pa, p2_ra, p2_p2, b_pa, b_ra, b_p2) = [
            s[i : i + 1] for i in range(10)
        ]
        alpha = rho / b_pa
        cross = ra_r - alpha * (ra_pa + p2_r) + alpha * alpha * p2_pa
        square = ra_ra - 2.0 * alpha * p2_ra + alpha * alpha * p2_p2
        omega = cross / square
        rho_next = -omega * (b_ra - alpha * b_p2)
        beta = rho_next / rho * (alpha / omega)
        return alpha, omega, beta, rho_next

    put_dots(1)
    sum_start(1)
    apply_local(PA2, 5)
    halo_start(5)
    sum_middle(1)
    halo_finish(5, PA3)
    apply_local(PA3, 6)
    halo_start(6)
    for x in range(8):
        vec[RA3, x] = vec[PA3, x] - be * (vec[V3, x] - om * vec[V4, x])
    halo_finish(6, PA4)

    alpha, omega, beta, rho = steps(1, rho)
    al, om, be = wide_of(alpha), wide_of(omega), wide_of(beta)
    for x in range(8):
        r0, r1, r2, r3 = [vec[i, x] for i in (R, RA, RA2, RA3)]
        p0, p1, p2, p3, p4 = [vec[i, x] for i in (PP, PA, PA2, PA3, PA4)]
        s0 = r0 - al * p1
        s1 = r1 - al * p2
        s2 = r2 - al * p3
        s3 = r3 - al * p4
        vec[X, x] = vec[X, x] + al * p0 + om * s0
        r0 = s0 - om * s1
        r1 = s1 - om * s2
        r2 = s2 - om * s3
        vec[R, x] = r0
        vec[RA, x] = r1
        vec[PP, x] = r0 + be * (p0 - om * p1)
        vec[PA, x] = r1 + be * (p1 - om * p2)
        vec[PA2, x] = r2 + be * (p2 - om * p3)

    put_dots(2)
    sum_start(2)
    sum_middle(2)
    alpha, omega, _, _ = steps(2, rho)
    al, om = wide_of(alpha), wide_of(omega)
    for x in range(8):
        s0 = vec[R, x] - al * vec[PA, x]
        s1 = vec[RA, x] - al * vec[PA2, x]
        adj_ref[x] = vec[X, x] + al * vec[PP, x] + om * s0
        res_ref[x] = s0 - om * s1

    pltpu.make_async_copy(xr, xr, send_x).wait()
    pltpu.make_async_copy(yr, yr, send_y).wait()
    pltpu.make_async_copy(cr, cr, send_c).wait()
    sent_1 = buf1.at[:, pl.ds(0, nx - 1)]
    pltpu.make_async_copy(sent_1, sent_1, send_1).wait()
    sent_2 = buf2.at[:, pl.ds(0, ny - 1)]
    pltpu.make_async_copy(sent_2, sent_2, send_2).wait()


def constants(nz):
    w = np.array(gll_weights)
    wz = np.tile(w, nz // 8)
    node = np.arange(nz) % 8
    elem = np.arange(nz) // 8
    shared = ((node == 7) & (elem < nz // 8 - 1)) | ((node == 0) & (elem > 0))
    inv_z = np.where(shared, 0.5, 1.0)
    planes = np.stack(
        [
            w[:, None] * wz[None, :],
            np.broadcast_to(inv_z, (8, nz)),
            np.broadcast_to(w[:, None], (8, nz)),
            np.broadcast_to(wz, (8, nz)),
        ]
    ).astype(np.float32)
    block = np.kron(np.eye(16), D)
    mats = np.stack([block.T, block]).astype(np.float32)
    along_y = np.kron(np.eye(8), D)
    kmat = np.stack([along_y, along_y.T]).astype(np.float32)
    return mats, kmat, planes


def solution(mesh):
    nx, ny = mesh.shape["gx"], mesh.shape["gy"]

    def per_device(source, conductivity, robin_flags, htc_class, htc_table):
        nz = source.shape[2]
        ez = robin_flags.shape[2]
        mats, kmat, planes = constants(nz)
        any_spec = pl.BlockSpec(memory_space=pl.ANY)
        vm = pltpu.VMEM
        dma = pltpu.SemaphoreType.DMA
        field = (8, 8, nz)
        return pl.pallas_call(
            functools.partial(kernel, nx, ny, nz),
            out_shape=(jax.ShapeDtypeStruct(field, f32), jax.ShapeDtypeStruct(field, f32)),
            in_specs=[any_spec] * 4
            + [pl.BlockSpec(memory_space=pltpu.SMEM)]
            + [any_spec] * 3,
            out_specs=(pl.BlockSpec(memory_space=pltpu.VMEM),) * 2,
            scratch_shapes=[
                vm(field, f32),
                vm(field, f32),
                vm((1, ez), jnp.int32),
                vm((1, ez), jnp.int32),
                vm((2, 128, 128), f32),
                vm((2, 64, 64), f32),
                vm((4, 8, nz), f32),
                vm(field, f32),
                vm(field, f32),
                vm((ROUNDS,) + field, f32),
                vm((15,) + field, f32),
                vm((ROUNDS, 2, 8, nz), f32),
                vm((ROUNDS, 2, 8, nz), f32),
                vm((ROUNDS, 4, 1, nz), f32),
                vm((ROUNDS, 2, 8, nz), f32),
                vm((ROUNDS, 4, 1, nz), f32),
                vm((SUMS, 128, 128), f32),
                vm((SUMS, 1, 128), f32),
                vm((SUMS, 1, 128), f32),
                vm((SUMS, nx, 1, 128), f32),
                vm((SUMS, ny, 1, 128), f32),
                dma((7,)),
                dma,
                dma,
                dma,
                dma((ROUNDS,)),
                dma((ROUNDS,)),
                dma((ROUNDS,)),
                dma,
                dma,
                dma((SUMS,)),
                dma((SUMS,)),
            ],
            compiler_params=pltpu.CompilerParams(collective_id=0, has_side_effects=True),
        )(
            source,
            conductivity,
            robin_flags.reshape(1, ez),
            htc_class.reshape(1, ez),
            htc_table,
            mats,
            kmat,
            planes,
        )

    return jax.shard_map(
        per_device,
        mesh=mesh,
        in_specs=(
            P("gx", "gy", None),
            P("gx", "gy", None),
            P("gx", "gy", None),
            P("gx", "gy", None),
            P(),
        ),
        out_specs=(P("gx", "gy", None), P("gx", "gy", None)),
        check_vma=False,
    )
```

time: 1220 us -> 70.3 us (0.06)
  blocking collectives: 816 us -> 0 us
  local copies, waits for them, and re-layouts: 218 us -> 2.26 us
  Pallas kernels: 0 us -> 67.2 us
  starting transfers between devices: 64.5 us -> 0 us
  other arithmetic: 46.8 us -> 0 us
  waiting for transfers between devices: 40.5 us -> 0 us
  between operations: 17.7 us -> 0.65 us
    psum x8 -> x0, blocking collectives: 816 us -> none  [the longest x3 313 us: per_device(): lax.psum((local_inner(applied_half, half_resid), local_inner(applied_half...]
    scatter x14 -> x0, local copies, waits for them, and re-layouts: 197 us -> none  [fold_inside(): blocks = blocks.at[:-1, 7].set(shared).at[1:, 0].set(shared)]
    pallas_call x0 -> x1, Pallas kernels: none -> 67.2 us  [per_device(): pl.pallas_call(functools.partial(kernel, nx, ny, nz), out_shape=(jax.Shap...]
    ppermute x28 -> x0, starting transfers between devices: 64.5 us -> none  [the longest x14 39.1 us: extended(): lax.ppermute(lax.slice_in_dim(block, block.shape[dim] - width, None, axis...]
    ppermute x28 -> x0, waiting for transfers between devices: 40.5 us -> none  [the longest x14 40.5 us: extended(): lax.ppermute(lax.slice_in_dim(block, 0, width, axis=dim), axis, backward)]
    another operation x12 -> x0, other arithmetic: 36.8 us -> none
    reshape x14 -> x0, local copies, waits for them, and re-layouts: 16.3 us -> none  [the longest x7 8.32 us: fold_inside(): return jnp.moveaxis(blocks.reshape(extent), 0, which_axis)]
  transfers between devices with their start and end apart: 28 -> 0, of which waited for: 13 -> 0; matrix products, arithmetic and copies ran while one was open for 0% -> 0% of each run, Pallas kernels for 0% -> 0%
where the time goes in v1:
time: 70.3 us; the launch traced here: 70.1 us
  Pallas kernels  67.2 us (96%)
  local copies, waits for them, and re-layouts  2.26 us (3%)
    pallas_call x1, Pallas kernels, per_device(): pl.pallas_call(functools.partial(kernel, nx, ny, nz), out_shape=(jax.Shap...  67.2 us
    unnamed x4, local copies, waits for them, and re-layouts  2.26 us

profile of v1, /device:TPU:1, one launch (start us, length us, event | category | flops | bytes accessed | tf_op | source)
XLA Modules:
  0.0 70.1 jit_solution(7018753525107497668)
XLA Ops:
  0.6 67.2 %shard_map.95 = (f32[8,8,512]{2,1,0:T(8,128)}, f32[8,8,512]{2,1,0:T(8,128)}) custom-call(f32[8,8,512]{2,1,0:T(8,128)} %src_hbm.1, f32[8,8,512]{2,1,0:T(8,128)} %cond_hbm.1, s32[1,64]{1,0:T(1,128)} %bitcast.2, s32[1,64]{1,0:T(1,128)} %bitcast.3, f32[4]{0:T(128)} %table_ref.1, f32[2,128,128]{2,1,0:T(8,128)} %constant.6.clone.mats_hbm, ...), custom_call_target="tpu_custom_call" | custom-call | tf_op jit(solution)/shard_map/pallas_call | solution.py:484
  67.9 0.0 copy-start
  67.9 1.6 %copy.12 = f32[8,8,512]{2,1,0:T(8,128)} copy(f32[8,8,512]{2,1,0:T(8,128)} %get-tuple-element.4) | data formatting | bytes 262144
  69.5 0.0 copy-done
  69.5 0.7 copy.13
Async XLA Ops:
  67.9 1.6 %copy-start = (f32[8,8,512]{2,1,0:T(8,128)S(1)}, f32[8,8,512]{2,1,0:T(8,128)}, u32[]{:S(2)}) copy-start(f32[8,8,512]{2,1,0:T(8,128)} %get-tuple-element.5) | copy-start | bytes 393220

commit v2 on v1

--- a/solution.py
+++ b/solution.py
@@ -69,10 +69,10 @@
 
 def kernel(
     nx, ny, nz,
-    src_hbm, cond_hbm, flags_hbm, class_hbm, table_ref, mats_hbm, kmat_hbm, planes_hbm,
+    src_hbm, cond_hbm, flags_hbm, class_hbm, table_hbm, mats_hbm, planes_hbm,
     adj_ref, res_ref,
-    src, wk, flags, classes, mats, kmat, planes, mass, im,
-    loc, vec, xr, yr, cr, ysend, csend,
+    src, cond, wk, wkt, flags, classes, table, mats, planes, mass, im,
+    loc, vec, tmp, xr, yr, cr, ysend,
     parts, msg1, msg2, buf1, buf2,
     in_sem, send_x, send_y, send_c, recv_x, recv_y, recv_c,
     send_1, send_2, recv_1, recv_2,
@@ -81,26 +81,26 @@
     gy = lax.axis_index("gy")
 
     def at_x(k):
-        return lax.rem(gx + (k % nx), nx)
+        return (gx + (k % nx)) & (nx - 1)
 
     def at_y(k):
-        return lax.rem(gy + (k % ny), ny)
+        return (gy + (k % ny)) & (ny - 1)
 
     loads = [
         pltpu.make_async_copy(a, b, in_sem.at[i])
         for i, (a, b) in enumerate(
             [
+                (src_hbm, src),
                 (planes_hbm, planes),
-                (src_hbm, src),
-                (cond_hbm, wk),
+                (cond_hbm, cond),
+                (mats_hbm, mats),
                 (flags_hbm, flags),
                 (class_hbm, classes),
-                (mats_hbm, mats),
-                (kmat_hbm, kmat),
+                (table_hbm, table),
             ]
         )
     ]
-    for c in loads:
+    for c in loads[:2]:
         c.start()
 
     barrier = pltpu.get_barrier_semaphore()
@@ -110,6 +110,8 @@
     peers += [(gx, at_y(k)) for k in order_y] + [(at_x(k), gy) for k in order_x]
     for peer in peers:
         pl.semaphore_signal(barrier, inc=1, device_id=peer, device_id_type=MESH)
+    for c in loads[2:]:
+        c.start()
 
     lane = lax.broadcasted_iota(jnp.int32, (8, nz), 1)
     node_z = lax.rem(lane, 8)
@@ -119,24 +121,35 @@
     zero = jnp.zeros((8, nz), f32)
     x_lo, x_hi = gx > 0, gx < nx - 1
     y_lo, y_hi = gy > 0, gy < ny - 1
+    row_t = lax.broadcasted_iota(jnp.int32, (8, 128), 0)
+    corner = ((row_t == 0) & x_lo) | ((row_t == 7) & x_hi)
+    tile0 = jnp.zeros((8, 128), f32)
+    chunks = [slice(128 * t, 128 * t + 128) for t in range(nz // 128)]
 
     def zfold(plane):
         up = pltpu.roll(plane, nz - 1, 1)
         dn = pltpu.roll(plane, 1, 1)
         return plane + jnp.where(join_up, up, jnp.where(join_dn, dn, zero))
 
+    nt = len(chunks)
+
+    def at(x):
+        return slice(8 * x, 8 * x + 8)
+
+    def get(ref, x):
+        return jnp.concatenate([ref[t, at(x), :] for t in range(nt)], axis=1)
+
+    def put(ref, x, plane):
+        for t, c in enumerate(chunks):
+            ref[t, at(x), :] = plane[:, c]
+
+    def across(y):
+        return pl.ds(y, 8, stride=8)
+
     for c in loads[:2]:
         c.wait()
     w_yz = planes[0]
     inv_z = planes[1]
-
-    def put_local(k, x, plane):
-        loc[k, x] = plane
-        ysend[k, 0, pl.ds(x, 1), :] = plane[0:1]
-        ysend[k, 1, pl.ds(x, 1), :] = plane[7:8]
-        if x in (0, 7):
-            csend[k, 0 if x == 0 else 2] = plane[0:1]
-            csend[k, 1 if x == 0 else 3] = plane[7:8]
 
     def halo_start(k):
         def send(s, d, ss, rs, peer):
@@ -145,38 +158,44 @@
                 device_id=peer, device_id_type=MESH,
             ).start()
 
-        for i, (dx, dy) in enumerate(((-1, -1), (-1, 1), (1, -1), (1, 1))):
-            send(csend.at[k, i], cr.at[k, 3 - i], send_c, recv_c.at[k], (at_x(dx), at_y(dy)))
+        for dx, dy in ((-1, -1), (-1, 1), (1, -1), (1, 1)):
+            mine = 56 * (dx > 0) + 7 * (dy > 0)
+            send(
+                loc.at[k, :, pl.ds(mine, 1), :],
+                cr.at[k, int(dy < 0), :, pl.ds(7 * (dx < 0), 1), :],
+                send_c, recv_c.at[k], (at_x(dx), at_y(dy)),
+            )
         for i, dy in enumerate((-1, 1)):
+            for t in range(nt):
+                ysend[k, i, t] = loc.at[k, t][across(7 * i), :]
             send(ysend.at[k, i], yr.at[k, 1 - i], send_y, recv_y.at[k], (gx, at_y(dy)))
         for i, dx in enumerate((-1, 1)):
-            send(loc.at[k, 7 * i], xr.at[k, 1 - i], send_x, recv_x.at[k], (at_x(dx), gy))
-
-    def halo_wait(k):
+            send(
+                loc.at[k, :, pl.ds(56 * i, 8), :], xr.at[k, 1 - i],
+                send_x, recv_x.at[k], (at_x(dx), gy),
+            )
+
+    def halo_finish(k, dst):
+        for t in range(nt):
+            vec[dst, t, 8:56, :] = loc[k, t, 8:56, :]
         pltpu.make_async_copy(xr.at[k], xr.at[k], recv_x.at[k]).wait()
+        for t in range(nt):
+            vec[dst, t, at(0), :] = loc[k, t, at(0), :] + jnp.where(x_lo, xr[k, 0, t], tile0)
+            vec[dst, t, at(7), :] = loc[k, t, at(7), :] + jnp.where(x_hi, xr[k, 1, t], tile0)
         pltpu.make_async_copy(yr.at[k], yr.at[k], recv_y.at[k]).wait()
-        pltpu.make_async_copy(cr.at[k], cr.at[k], recv_c.at[k]).wait()
-
-    def assembled_plane(k, x):
-        plane = loc[k, x]
-        lo = jnp.broadcast_to(yr[k, 0, pl.ds(x, 1), :], (8, nz))
-        hi = jnp.broadcast_to(yr[k, 1, pl.ds(x, 1), :], (8, nz))
-        if x in (0, 7):
-            i = 0 if x == 0 else 1
-            has = x_lo if x == 0 else x_hi
-            lo = lo + jnp.where(has, jnp.broadcast_to(cr[k, 2 * i], (8, nz)), zero)
-            hi = hi + jnp.where(has, jnp.broadcast_to(cr[k, 2 * i + 1], (8, nz)), zero)
-            plane = plane + jnp.where(has, xr[k, i], zero)
-        add = jnp.where((row == 0) & y_lo, lo, jnp.where((row == 7) & y_hi, hi, zero))
-        return plane + add
-
-    def halo_finish(k, dst):
-        halo_wait(k)
-        for x in range(8):
-            vec[dst, x] = assembled_plane(k, x)
+        lines = cr.at[k, 0, :, pl.ds(0, 4), :]
+        pltpu.make_async_copy(lines, lines, recv_c.at[k]).wait()
+        for i, has in enumerate((y_lo, y_hi)):
+            for t in range(nt):
+                add = yr[k, i, t] + jnp.where(corner, cr[k, i, t], tile0)
+                add = jnp.where(has, add, tile0)
+                vec.at[dst, t][across(7 * i), :] = vec.at[dst, t][across(7 * i), :] + add
 
     for x in range(8):
-        put_local(0, x, zfold(float(gll_weights[x]) * w_yz * src[x]))
+        put(loc.at[0], x, zfold(float(gll_weights[x]) * w_yz * src[x]))
+
+    pl.semaphore_wait(barrier, len(peers))
+    halo_start(0)
 
     for c in loads[2:]:
         c.wait()
@@ -184,11 +203,7 @@
     kinds = classes[...]
     coef = jnp.zeros(kinds.shape, f32)
     for i in range(4):
-        coef = coef + jnp.where(kinds == i, table_ref[i], 0.0)
-
-    pl.semaphore_wait(barrier, len(peers))
-    halo_start(0)
-
+        coef = coef + jnp.where(kinds == i, table[0, i], 0.0)
     edge = [gx == 0, gx == nx - 1, gy == 0, gy == ny - 1]
     faces = []
     for i in range(6):
@@ -221,35 +236,53 @@
         if x == 7:
             robin = robin + line(1) * w_yz
             inv = jnp.where(x_hi, 0.5 * inv_yz, inv_yz)
-        mass[x] = (mass_coef * wx) * w_yz + robin
-        im[x] = inv
-        wk[x] = (wx * w_yz) * wk[x]
-
-    chunks = [slice(128 * t, 128 * t + 128) for t in range(nz // 128)]
+        put(mass, x, (mass_coef * wx) * w_yz + robin)
+        put(im, x, inv)
+        put(wk, x, (wx * w_yz) * cond[x])
+    for t in range(nt):
+        for y in range(8):
+            wkt[t, at(y), :] = wk.at[t][across(y), :]
+
+    bf = jnp.bfloat16
+
+    def pieces(v):
+        h1 = v.astype(bf)
+        rest = v - h1.astype(f32)
+        h2 = rest.astype(bf)
+        h3 = (rest - h2.astype(f32)).astype(bf)
+        return jnp.concatenate([h1, h2], axis=1), jnp.concatenate([h3, h1], axis=1)
+
+    def along_z(v, i):
+        first, second = pieces(v)
+        one = jnp.dot(first, mats[i, 0], preferred_element_type=f32)
+        two = jnp.dot(second, mats[i, 1, :, 0:128], preferred_element_type=f32)
+        return one[:, 0:128] + (one[:, 128:256] + two)
 
     def apply_local(s, k):
-        v = [vec[s, x] for x in range(8)]
-        grad_x = along_planes(v, D)
-        flux_x = [
-            wk[x] * grad_x[x] - (scan_speed * float(gll_weights[x])) * (w_yz * v[x])
-            for x in range(8)
-        ]
-        back_x = along_planes(flux_x, D.T)
-        acc = [mass[x] * v[x] + back_x[x] for x in range(8)]
-        whole = vec[s].reshape(64, nz)
-        wk2 = wk[...].reshape(64, nz)
-        grad_y = jnp.dot(kmat[0], whole, precision=HIGHEST, preferred_element_type=f32)
-        back = jnp.dot(kmat[1], wk2 * grad_y, precision=HIGHEST, preferred_element_type=f32)
-        tall = jnp.concatenate([whole[:, c] for c in chunks], axis=0)
-        wk_t = jnp.concatenate([wk2[:, c] for c in chunks], axis=0)
-        grad_z = jnp.dot(tall, mats[0], precision=HIGHEST, preferred_element_type=f32)
-        back_z = jnp.dot(wk_t * grad_z, mats[1], precision=HIGHEST, preferred_element_type=f32)
-        back_z = jnp.concatenate(
-            [back_z[64 * t : 64 * t + 64] for t in range(len(chunks))], axis=1
-        )
-        back = (back + back_z).reshape(8, 8, nz)
+        rows = 64 * nt
+        grad_z = along_z(vec[s].reshape(rows, 128), 0)
+        back_z = along_z(wk[...].reshape(rows, 128) * grad_z, 1)
+        for t, c in enumerate(chunks):
+            turned = [vec.at[s, t][across(y), :] for y in range(8)]
+            grad = along_planes(turned, D)
+            back = along_planes([wkt[t, at(y), :] * grad[y] for y in range(8)], D.T)
+            for y in range(8):
+                tmp.at[t][across(y), :] = back[y]
+            v = [vec[s, t, at(x), :] for x in range(8)]
+            grad = along_planes(v, D)
+            flux = [
+                wk[t, at(x), :] * grad[x]
+                - (scan_speed * float(gll_weights[x])) * (w_yz[:, c] * v[x])
+                for x in range(8)
+            ]
+            back = along_planes(flux, D.T)
+            for x in range(8):
+                tmp[t, at(x), :] = tmp[t, at(x), :] + (mass[t, at(x), :] * v[x] + back[x])
         for x in range(8):
-            put_local(k, x, zfold(acc[x] + back[x]))
+            side = jnp.concatenate(
+                [back_z[64 * t + 8 * x : 64 * t + 8 * x + 8] for t in range(nt)], axis=1
+            )
+            put(loc.at[k], x, zfold(get(tmp, x) + side))
 
     parts[...] = jnp.zeros(parts.shape, f32)
     ones = jnp.ones((8, 128), f32)
@@ -259,10 +292,10 @@
         parts[j, 8 * d : 8 * d + 8, :] = sum(total[:, c] for c in chunks)
 
     def planes_of(s):
-        return [vec[s, x] for x in range(8)]
+        return [get(vec.at[s], x) for x in range(8)]
 
     def weighted(v):
-        return [im[x] * v[x] for x in range(8)]
+        return [get(im, x) * v[x] for x in range(8)]
 
     def sum_start(j):
         rows = lax.dot_general(
@@ -324,14 +357,14 @@
     put_dot(0, 1, weighted(planes_of(B)), v1)
     put_dot(0, 2, weighted(v1), v1)
     halo_finish(2, V2)
+    apply_local(V2, 3)
+    halo_start(3)
     v2 = planes_of(V2)
     v2w = weighted(v2)
     put_dot(0, 3, v2w, planes_of(B))
     put_dot(0, 4, v2w, planes_of(V1))
     put_dot(0, 5, v2w, v2)
     sum_start(0)
-    apply_local(V2, 3)
-    halo_start(3)
     sum_middle(0)
     halo_finish(3, V3)
     apply_local(V3, 4)
@@ -350,21 +383,21 @@
     rho = rho_next
     al, om, be = wide_of(alpha), wide_of(omega), wide_of(beta)
     for x in range(8):
-        b, v1, v2, v3, v4 = [vec[i, x] for i in (B, V1, V2, V3, V4)]
+        b, v1, v2, v3, v4 = [get(vec.at[i], x) for i in (B, V1, V2, V3, V4)]
         s0 = b - al * v1
         s1 = v1 - al * v2
         s2 = v2 - al * v3
         s3 = v3 - al * v4
-        vec[X, x] = al * b + om * s0
+        put(vec.at[X], x, al * b + om * s0)
         r0 = s0 - om * s1
         r1 = s1 - om * s2
         r2 = s2 - om * s3
-        vec[R, x] = r0
-        vec[RA, x] = r1
-        vec[RA2, x] = r2
-        vec[PP, x] = r0 + be * (b - om * v1)
-        vec[PA, x] = r1 + be * (v1 - om * v2)
-        vec[PA2, x] = r2 + be * (v2 - om * v3)
+        put(vec.at[R], x, r0)
+        put(vec.at[RA], x, r1)
+        put(vec.at[RA2], x, r2)
+        put(vec.at[PP], x, r0 + be * (b - om * v1))
+        put(vec.at[PA], x, r1 + be * (v1 - om * v2))
+        put(vec.at[PA2], x, r2 + be * (v2 - om * v3))
 
     def put_dots(j):
         ra = planes_of(RA)
@@ -397,36 +430,36 @@
         beta = rho_next / rho * (alpha / omega)
         return alpha, omega, beta, rho_next
 
+    apply_local(PA2, 5)
+    halo_start(5)
     put_dots(1)
     sum_start(1)
-    apply_local(PA2, 5)
-    halo_start(5)
     sum_middle(1)
     halo_finish(5, PA3)
     apply_local(PA3, 6)
     halo_start(6)
     for x in range(8):
-        vec[RA3, x] = vec[PA3, x] - be * (vec[V3, x] - om * vec[V4, x])
+        put(vec.at[RA3], x, get(vec.at[PA3], x) - be * (get(vec.at[V3], x) - om * get(vec.at[V4], x)))
     halo_finish(6, PA4)
 
     alpha, omega, beta, rho = steps(1, rho)
     al, om, be = wide_of(alpha), wide_of(omega), wide_of(beta)
     for x in range(8):
-        r0, r1, r2, r3 = [vec[i, x] for i in (R, RA, RA2, RA3)]
-        p0, p1, p2, p3, p4 = [vec[i, x] for i in (PP, PA, PA2, PA3, PA4)]
+        r0, r1, r2, r3 = [get(vec.at[i], x) for i in (R, RA, RA2, RA3)]
+        p0, p1, p2, p3, p4 = [get(vec.at[i], x) for i in (PP, PA, PA2, PA3, PA4)]
         s0 = r0 - al * p1
         s1 = r1 - al * p2
         s2 = r2 - al * p3
         s3 = r3 - al * p4
-        vec[X, x] = vec[X, x] + al * p0 + om * s0
+        put(vec.at[X], x, get(vec.at[X], x) + al * p0 + om * s0)
         r0 = s0 - om * s1
         r1 = s1 - om * s2
         r2 = s2 - om * s3
-        vec[R, x] = r0
-        vec[RA, x] = r1
-        vec[PP, x] = r0 + be * (p0 - om * p1)
-        vec[PA, x] = r1 + be * (p1 - om * p2)
-        vec[PA2, x] = r2 + be * (p2 - om * p3)
+        put(vec.at[R], x, r0)
+        put(vec.at[RA], x, r1)
+        put(vec.at[PP], x, r0 + be * (p0 - om * p1))
+        put(vec.at[PA], x, r1 + be * (p1 - om * p2))
+        put(vec.at[PA2], x, r2 + be * (p2 - om * p3))
 
     put_dots(2)
     sum_start(2)
@@ -434,14 +467,15 @@
     alpha, omega, _, _ = steps(2, rho)
     al, om = wide_of(alpha), wide_of(omega)
     for x in range(8):
-        s0 = vec[R, x] - al * vec[PA, x]
-        s1 = vec[RA, x] - al * vec[PA2, x]
-        adj_ref[x] = vec[X, x] + al * vec[PP, x] + om * s0
+        s0 = get(vec.at[R], x) - al * get(vec.at[PA], x)
+        s1 = get(vec.at[RA], x) - al * get(vec.at[PA2], x)
+        adj_ref[x] = get(vec.at[X], x) + al * get(vec.at[PP], x) + om * s0
         res_ref[x] = s0 - om * s1
 
     pltpu.make_async_copy(xr, xr, send_x).wait()
     pltpu.make_async_copy(yr, yr, send_y).wait()
-    pltpu.make_async_copy(cr, cr, send_c).wait()
+    lines = cr.at[:, 0, :, pl.ds(0, 4), :]
+    pltpu.make_async_copy(lines, lines, send_c).wait()
     sent_1 = buf1.at[:, pl.ds(0, nx - 1)]
     pltpu.make_async_copy(sent_1, sent_1, send_1).wait()
     sent_2 = buf2.at[:, pl.ds(0, ny - 1)]
@@ -463,11 +497,26 @@
             np.broadcast_to(wz, (8, nz)),
         ]
     ).astype(np.float32)
-    block = np.kron(np.eye(16), D)
-    mats = np.stack([block.T, block]).astype(np.float32)
-    along_y = np.kron(np.eye(8), D)
-    kmat = np.stack([along_y, along_y.T]).astype(np.float32)
-    return mats, kmat, planes
+    mats = []
+    for small in (D.T, D):
+        rest = np.kron(np.eye(16), small).astype(np.float32)
+        parts = []
+        for _ in range(3):
+            part = rest.astype(jnp.bfloat16)
+            parts.append(part)
+            rest = rest - part.astype(np.float32)
+        d1, d2, d3 = parts
+        both = np.concatenate([d1, d2], axis=1)
+        last = np.concatenate([d1, d3], axis=0)
+        mats.append(
+            np.stack(
+                [
+                    np.concatenate([both, both], axis=0),
+                    np.concatenate([last, np.zeros_like(last)], axis=1),
+                ]
+            )
+        )
+    return np.stack(mats), planes
 
 
 def solution(mesh):
@@ -476,35 +525,37 @@
     def per_device(source, conductivity, robin_flags, htc_class, htc_table):
         nz = source.shape[2]
         ez = robin_flags.shape[2]
-        mats, kmat, planes = constants(nz)
+        mats, planes = constants(nz)
         any_spec = pl.BlockSpec(memory_space=pl.ANY)
         vm = pltpu.VMEM
         dma = pltpu.SemaphoreType.DMA
         field = (8, 8, nz)
+        nt = nz // 128
+        flat = (nt, 64, 128)
         return pl.pallas_call(
             functools.partial(kernel, nx, ny, nz),
             out_shape=(jax.ShapeDtypeStruct(field, f32), jax.ShapeDtypeStruct(field, f32)),
-            in_specs=[any_spec] * 4
-            + [pl.BlockSpec(memory_space=pltpu.SMEM)]
-            + [any_spec] * 3,
+            in_specs=[any_spec] * 7,
             out_specs=(pl.BlockSpec(memory_space=pltpu.VMEM),) * 2,
             scratch_shapes=[
                 vm(field, f32),
                 vm(field, f32),
+                vm(flat, f32),
+                vm(flat, f32),
                 vm((1, ez), jnp.int32),
                 vm((1, ez), jnp.int32),
-                vm((2, 128, 128), f32),
-                vm((2, 64, 64), f32),
+                pltpu.SMEM((1, 4), f32),
+                vm((2, 2, 256, 256), jnp.bfloat16),
                 vm((4, 8, nz), f32),
-                vm(field, f32),
-                vm(field, f32),
-                vm((ROUNDS,) + field, f32),
-                vm((15,) + field, f32),
-                vm((ROUNDS, 2, 8, nz), f32),
-                vm((ROUNDS, 2, 8, nz), f32),
-                vm((ROUNDS, 4, 1, nz), f32),
-                vm((ROUNDS, 2, 8, nz), f32),
-                vm((ROUNDS, 4, 1, nz), f32),
+                vm(flat, f32),
+                vm(flat, f32),
+                vm((ROUNDS,) + flat, f32),
+                vm((15,) + flat, f32),
+                vm(flat, f32),
+                vm((ROUNDS, 2, nt, 8, 128), f32),
+                vm((ROUNDS, 2, nt, 8, 128), f32),
+                vm((ROUNDS, 2, nt, 8, 128), f32),
+                vm((ROUNDS, 2, nt, 8, 128), f32),
                 vm((SUMS, 128, 128), f32),
                 vm((SUMS, 1, 128), f32),
                 vm((SUMS, 1, 128), f32),
@@ -528,9 +579,8 @@
             conductivity,
             robin_flags.reshape(1, ez),
             htc_class.reshape(1, ez),
-            htc_table,
+            htc_table.reshape(1, 4),
             mats,
-            kmat,
             planes,
         )
 

time: 70.3 us -> 67.6 us (0.962)
  Pallas kernels: 67.2 us -> 64.6 us
    pallas_call x1, Pallas kernels: 67.2 us -> 64.6 us  [per_device(): pl.pallas_call(functools.partial(kernel, nx, ny, nz), out_shape=(jax.Shap...]
where the time goes in v2:
time: 67.6 us; the launch traced here: 67.5 us
  Pallas kernels  64.6 us (96%)
  local copies, waits for them, and re-layouts  2.26 us (3%)
    pallas_call x1, Pallas kernels, per_device(): pl.pallas_call(functools.partial(kernel, nx, ny, nz), out_shape=(jax.Shap...  64.6 us
    unnamed x4, local copies, waits for them, and re-layouts  2.26 us

profile of v2, /device:TPU:1, one launch (start us, length us, event | category | flops | bytes accessed | tf_op | source)
XLA Modules:
  0.0 67.5 jit_solution(5418694988485551909)
XLA Ops:
  0.6 64.6 %shard_map.86 = (f32[8,8,512]{2,1,0:T(8,128)}, f32[8,8,512]{2,1,0:T(8,128)}) custom-call(f32[8,8,512]{2,1,0:T(8,128)} %src_hbm.1, f32[8,8,512]{2,1,0:T(8,128)} %cond_hbm.1, s32[1,64]{1,0:T(1,128)} %bitcast.3, s32[1,64]{1,0:T(1,128)} %bitcast.4, f32[1,4]{1,0:T(1,128)} %bitcast.5, bf16[2,2,256,256]{3,2,1,0:T(8,128)(2,1)} %constant.4.clone.mats_hbm, ...), custom_call_target="tpu_custom_call" | custom-call | tf_op jit(solution)/shard_map/pallas_call | solution.py:535
  65.2 0.0 copy-start
  65.2 1.6 %copy.11 = f32[8,8,512]{2,1,0:T(8,128)} copy(f32[8,8,512]{2,1,0:T(8,128)} %get-tuple-element.4) | data formatting | bytes 262144
  66.8 0.0 copy-done
  66.8 0.7 copy.12
Async XLA Ops:
  65.2 1.6 %copy-start = (f32[8,8,512]{2,1,0:T(8,128)S(1)}, f32[8,8,512]{2,1,0:T(8,128)}, u32[]{:S(2)}) copy-start(f32[8,8,512]{2,1,0:T(8,128)} %get-tuple-element.5) | copy-start | bytes 393220

commit v3 on v2

--- a/solution.py
+++ b/solution.py
@@ -67,12 +67,20 @@
     return out
 
 
+def ends(planes, mat):
+    even = [planes[b] + planes[7 - b] for b in range(4)]
+    odd = [planes[b] - planes[7 - b] for b in range(4)]
+    p = sum(float(0.5 * (mat[0, b] + mat[0, 7 - b])) * even[b] for b in range(4))
+    q = sum(float(0.5 * (mat[0, b] - mat[0, 7 - b])) * odd[b] for b in range(4))
+    return p + q, q - p
+
+
 def kernel(
     nx, ny, nz,
     src_hbm, cond_hbm, flags_hbm, class_hbm, table_hbm, mats_hbm, planes_hbm,
-    adj_ref, res_ref,
-    src, cond, wk, wkt, flags, classes, table, mats, planes, mass, im,
-    loc, vec, tmp, xr, yr, cr, ysend,
+    x_out, pp_out, r_out, pa_out, ra_out, pa2_out, al_out, om_out,
+    src, cond, w2, wk, wkt, flags, classes, table, mats, planes, mass, im,
+    loc, vec, tmp, fx, fy, ywk, xr, yr, cr, ysend,
     parts, msg1, msg2, buf1, buf2,
     in_sem, send_x, send_y, send_c, recv_x, recv_y, recv_c,
     send_1, send_2, recv_1, recv_2,
@@ -151,24 +159,23 @@
     w_yz = planes[0]
     inv_z = planes[1]
 
-    def halo_start(k):
-        def send(s, d, ss, rs, peer):
-            pltpu.make_async_remote_copy(
-                src_ref=s, dst_ref=d, send_sem=ss, recv_sem=rs,
-                device_id=peer, device_id_type=MESH,
-            ).start()
-
+    def send(s, d, ss, rs, peer):
+        pltpu.make_async_remote_copy(
+            src_ref=s, dst_ref=d, send_sem=ss, recv_sem=rs,
+            device_id=peer, device_id_type=MESH,
+        ).start()
+
+    def y_start(k):
         for dx, dy in ((-1, -1), (-1, 1), (1, -1), (1, 1)):
-            mine = 56 * (dx > 0) + 7 * (dy > 0)
             send(
-                loc.at[k, :, pl.ds(mine, 1), :],
+                ysend.at[k, int(dy > 0), :, pl.ds(7 * (dx > 0), 1), :],
                 cr.at[k, int(dy < 0), :, pl.ds(7 * (dx < 0), 1), :],
                 send_c, recv_c.at[k], (at_x(dx), at_y(dy)),
             )
         for i, dy in enumerate((-1, 1)):
-            for t in range(nt):
-                ysend[k, i, t] = loc.at[k, t][across(7 * i), :]
             send(ysend.at[k, i], yr.at[k, 1 - i], send_y, recv_y.at[k], (gx, at_y(dy)))
+
+    def x_start(k):
         for i, dx in enumerate((-1, 1)):
             send(
                 loc.at[k, :, pl.ds(56 * i, 8), :], xr.at[k, 1 - i],
@@ -194,8 +201,12 @@
     for x in range(8):
         put(loc.at[0], x, zfold(float(gll_weights[x]) * w_yz * src[x]))
 
+    for i in (0, 1):
+        for t in range(nt):
+            ysend[0, i, t] = loc.at[0, t][across(7 * i), :]
     pl.semaphore_wait(barrier, len(peers))
-    halo_start(0)
+    y_start(0)
+    x_start(0)
 
     for c in loads[2:]:
         c.wait()
@@ -238,10 +249,13 @@
             inv = jnp.where(x_hi, 0.5 * inv_yz, inv_yz)
         put(mass, x, (mass_coef * wx) * w_yz + robin)
         put(im, x, inv)
+        w2[x] = (scan_speed * wx) * w_yz
         put(wk, x, (wx * w_yz) * cond[x])
     for t in range(nt):
         for y in range(8):
             wkt[t, at(y), :] = wk.at[t][across(y), :]
+        for i in (0, 1):
+            ywk[pl.ds(8 * (i * nt + t), 8), :] = wk.at[t][across(7 * i), :]
 
     bf = jnp.bfloat16
 
@@ -258,31 +272,51 @@
         two = jnp.dot(second, mats[i, 1, :, 0:128], preferred_element_type=f32)
         return one[:, 0:128] + (one[:, 128:256] + two)
 
-    def apply_local(s, k):
-        rows = 64 * nt
-        grad_z = along_z(vec[s].reshape(rows, 128), 0)
-        back_z = along_z(wk[...].reshape(rows, 128) * grad_z, 1)
-        for t, c in enumerate(chunks):
+    def apply_edges(s, k):
+        rows = jnp.concatenate(
+            [vec.at[s, t][across(7 * i), :] for i in (0, 1) for t in range(nt)], axis=0
+        )
+        face_z = along_z(ywk[...] * along_z(rows, 0), 1)
+        face_y = [[], []]
+        for t in range(nt):
             turned = [vec.at[s, t][across(y), :] for y in range(8)]
             grad = along_planes(turned, D)
-            back = along_planes([wkt[t, at(y), :] * grad[y] for y in range(8)], D.T)
+            flux = [wkt[t, at(y), :] * grad[y] for y in range(8)]
+            for y in range(8):
+                fy[t, at(y), :] = flux[y]
+            for i, end in enumerate(ends(flux, D.T)):
+                face_y[i].append(end)
+            v = [vec[s, t, at(x), :] for x in range(8)]
+            grad = along_planes(v, D)
+            flux = [wk[t, at(x), :] * grad[x] - w2[x, :, chunks[t]] * v[x] for x in range(8)]
+            back = along_planes(flux, D.T)
+            for x in range(8):
+                fx[t, at(x), :] = mass[t, at(x), :] * v[x] + back[x]
+        for i in (0, 1):
+            face = [
+                fx.at[t][across(7 * i), :]
+                + face_y[i][t]
+                + face_z[8 * (i * nt + t) : 8 * (i * nt + t) + 8]
+                for t in range(nt)
+            ]
+            face = zfold(jnp.concatenate(face, axis=1))
+            for t, c in enumerate(chunks):
+                ysend[k, i, t] = face[:, c]
+        y_start(k)
+
+    def apply_rest(s, k):
+        grad_z = along_z(vec[s].reshape(64 * nt, 128), 0)
+        back_z = along_z(wk[...].reshape(64 * nt, 128) * grad_z, 1)
+        for t in range(nt):
+            back = along_planes([fy[t, at(y), :] for y in range(8)], D.T)
             for y in range(8):
                 tmp.at[t][across(y), :] = back[y]
-            v = [vec[s, t, at(x), :] for x in range(8)]
-            grad = along_planes(v, D)
-            flux = [
-                wk[t, at(x), :] * grad[x]
-                - (scan_speed * float(gll_weights[x])) * (w_yz[:, c] * v[x])
-                for x in range(8)
-            ]
-            back = along_planes(flux, D.T)
-            for x in range(8):
-                tmp[t, at(x), :] = tmp[t, at(x), :] + (mass[t, at(x), :] * v[x] + back[x])
         for x in range(8):
             side = jnp.concatenate(
                 [back_z[64 * t + 8 * x : 64 * t + 8 * x + 8] for t in range(nt)], axis=1
             )
-            put(loc.at[k], x, zfold(get(tmp, x) + side))
+            put(loc.at[k], x, zfold(get(tmp, x) + get(fx, x) + side))
+        x_start(k)
 
     parts[...] = jnp.zeros(parts.shape, f32)
     ones = jnp.ones((8, 128), f32)
@@ -342,33 +376,33 @@
     def wide_of(scalar):
         return jnp.broadcast_to(jnp.concatenate([scalar] * len(chunks), axis=1), (8, nz))
 
-    B, V1, V2, V3, V4, R, RA, RA2, RA3, PP, PA, PA2, PA3, PA4, X = range(15)
+    B, V1, V2, V3, V4, R, RA, RA2, RA3, PP, PA, PA2, PA3, PA4, X, NR, NPA = range(17)
 
     halo_finish(0, B)
-    apply_local(B, 1)
-    halo_start(1)
+    apply_edges(B, 1)
+    apply_rest(B, 1)
     b = planes_of(B)
     bw = weighted(b)
     put_dot(0, 0, bw, b)
     halo_finish(1, V1)
-    apply_local(V1, 2)
-    halo_start(2)
+    apply_edges(V1, 2)
+    apply_rest(V1, 2)
     v1 = planes_of(V1)
     put_dot(0, 1, weighted(planes_of(B)), v1)
     put_dot(0, 2, weighted(v1), v1)
     halo_finish(2, V2)
-    apply_local(V2, 3)
-    halo_start(3)
+    apply_edges(V2, 3)
     v2 = planes_of(V2)
     v2w = weighted(v2)
     put_dot(0, 3, v2w, planes_of(B))
     put_dot(0, 4, v2w, planes_of(V1))
     put_dot(0, 5, v2w, v2)
     sum_start(0)
+    apply_rest(V2, 3)
     sum_middle(0)
     halo_finish(3, V3)
-    apply_local(V3, 4)
-    halo_start(4)
+    apply_edges(V3, 4)
+    apply_rest(V3, 4)
     halo_finish(4, V4)
 
     s = sum_finish(0)
@@ -383,36 +417,39 @@
     rho = rho_next
     al, om, be = wide_of(alpha), wide_of(omega), wide_of(beta)
     for x in range(8):
-        b, v1, v2, v3, v4 = [get(vec.at[i], x) for i in (B, V1, V2, V3, V4)]
+        v2, v3, v4 = [get(vec.at[i], x) for i in (V2, V3, V4)]
+        s2 = v2 - al * v3
+        r2 = s2 - om * (v3 - al * v4)
+        put(vec.at[RA2], x, r2)
+        put(vec.at[PA2], x, r2 + be * (v2 - om * v3))
+    apply_edges(PA2, 5)
+    for x in range(8):
+        b, v1, v2, v3 = [get(vec.at[i], x) for i in (B, V1, V2, V3)]
         s0 = b - al * v1
         s1 = v1 - al * v2
-        s2 = v2 - al * v3
-        s3 = v3 - al * v4
         put(vec.at[X], x, al * b + om * s0)
         r0 = s0 - om * s1
-        r1 = s1 - om * s2
-        r2 = s2 - om * s3
+        r1 = s1 - om * (v2 - al * v3)
         put(vec.at[R], x, r0)
         put(vec.at[RA], x, r1)
-        put(vec.at[RA2], x, r2)
         put(vec.at[PP], x, r0 + be * (b - om * v1))
         put(vec.at[PA], x, r1 + be * (v1 - om * v2))
-        put(vec.at[PA2], x, r2 + be * (v2 - om * v3))
 
     def put_dots(j):
+        r_slot, pa_slot = (R, PA) if j == 1 else (NR, NPA)
         ra = planes_of(RA)
         raw = weighted(ra)
-        put_dot(j, 0, raw, planes_of(R))
-        put_dot(j, 1, raw, planes_of(PA))
+        put_dot(j, 0, raw, planes_of(r_slot))
+        put_dot(j, 1, raw, planes_of(pa_slot))
         put_dot(j, 2, raw, ra)
         pa2 = planes_of(PA2)
         pa2w = weighted(pa2)
-        put_dot(j, 3, pa2w, planes_of(R))
-        put_dot(j, 4, pa2w, planes_of(PA))
+        put_dot(j, 3, pa2w, planes_of(r_slot))
+        put_dot(j, 4, pa2w, planes_of(pa_slot))
         put_dot(j, 5, pa2w, ra)
         put_dot(j, 6, pa2w, pa2)
         bw = weighted(planes_of(B))
-        put_dot(j, 7, bw, planes_of(PA))
+        put_dot(j, 7, bw, planes_of(pa_slot))
         if j == 1:
             put_dot(j, 8, bw, ra)
             put_dot(j, 9, bw, pa2)
@@ -430,14 +467,13 @@
         beta = rho_next / rho * (alpha / omega)
         return alpha, omega, beta, rho_next
 
-    apply_local(PA2, 5)
-    halo_start(5)
     put_dots(1)
     sum_start(1)
+    apply_rest(PA2, 5)
     sum_middle(1)
     halo_finish(5, PA3)
-    apply_local(PA3, 6)
-    halo_start(6)
+    apply_edges(PA3, 6)
+    apply_rest(PA3, 6)
     for x in range(8):
         put(vec.at[RA3], x, get(vec.at[PA3], x) - be * (get(vec.at[V3], x) - om * get(vec.at[V4], x)))
     halo_finish(6, PA4)
@@ -451,26 +487,28 @@
         s1 = r1 - al * p2
         s2 = r2 - al * p3
         s3 = r3 - al * p4
-        put(vec.at[X], x, get(vec.at[X], x) + al * p0 + om * s0)
         r0 = s0 - om * s1
         r1 = s1 - om * s2
         r2 = s2 - om * s3
-        put(vec.at[R], x, r0)
+        put(vec.at[NR], x, r0)
         put(vec.at[RA], x, r1)
-        put(vec.at[PP], x, r0 + be * (p0 - om * p1))
-        put(vec.at[PA], x, r1 + be * (p1 - om * p2))
+        put(vec.at[NPA], x, r1 + be * (p1 - om * p2))
         put(vec.at[PA2], x, r2 + be * (p2 - om * p3))
 
     put_dots(2)
     sum_start(2)
+    for x in range(8):
+        r, p0, p1, r0 = [get(vec.at[i], x) for i in (R, PP, PA, NR)]
+        x_out[x] = get(vec.at[X], x) + al * p0 + om * (r - al * p1)
+        pp_out[x] = r0 + be * (p0 - om * p1)
+        r_out[x] = r0
+        pa_out[x] = get(vec.at[NPA], x)
+        ra_out[x] = get(vec.at[RA], x)
+        pa2_out[x] = get(vec.at[PA2], x)
     sum_middle(2)
     alpha, omega, _, _ = steps(2, rho)
-    al, om = wide_of(alpha), wide_of(omega)
-    for x in range(8):
-        s0 = get(vec.at[R], x) - al * get(vec.at[PA], x)
-        s1 = get(vec.at[RA], x) - al * get(vec.at[PA2], x)
-        adj_ref[x] = get(vec.at[X], x) + al * get(vec.at[PP], x) + om * s0
-        res_ref[x] = s0 - om * s1
+    al_out[...] = wide_of(alpha)
+    om_out[...] = wide_of(omega)
 
     pltpu.make_async_copy(xr, xr, send_x).wait()
     pltpu.make_async_copy(yr, yr, send_y).wait()
@@ -532,12 +570,13 @@
         field = (8, 8, nz)
         nt = nz // 128
         flat = (nt, 64, 128)
-        return pl.pallas_call(
+        x, pp, r, pa, ra, pa2, alpha, omega = pl.pallas_call(
             functools.partial(kernel, nx, ny, nz),
-            out_shape=(jax.ShapeDtypeStruct(field, f32), jax.ShapeDtypeStruct(field, f32)),
+            out_shape=(pltpu.VMEM(field, f32),) * 6 + (pltpu.VMEM((8, nz), f32),) * 2,
             in_specs=[any_spec] * 7,
-            out_specs=(pl.BlockSpec(memory_space=pltpu.VMEM),) * 2,
+            out_specs=(pl.BlockSpec(memory_space=pltpu.VMEM),) * 8,
             scratch_shapes=[
+                vm(field, f32),
                 vm(field, f32),
                 vm(field, f32),
                 vm(flat, f32),
@@ -550,8 +589,11 @@
                 vm(flat, f32),
                 vm(flat, f32),
                 vm((ROUNDS,) + flat, f32),
-                vm((15,) + flat, f32),
+                vm((17,) + flat, f32),
                 vm(flat, f32),
+                vm(flat, f32),
+                vm(flat, f32),
+                vm((16 * nt, 128), f32),
                 vm((ROUNDS, 2, nt, 8, 128), f32),
                 vm((ROUNDS, 2, nt, 8, 128), f32),
                 vm((ROUNDS, 2, nt, 8, 128), f32),
@@ -583,6 +625,8 @@
             mats,
             planes,
         )
+        half = r - alpha * pa
+        return x + alpha * pp + omega * half, half - omega * (ra - alpha * pa2)
 
     return jax.shard_map(
         per_device,

time: 67.6 us -> 65.5 us (0.969)
  local copies, waits for them, and re-layouts: 2.26 us -> 0 us
  other arithmetic: 0 us -> 0.77 us
    unnamed x4 -> x0, local copies, waits for them, and re-layouts: 2.26 us -> none
    sub x0 -> x1, other arithmetic: none -> 0.77 us  [per_device(): return (x + alpha * pp + omega * half, half - omega * (ra - alpha * pa2))]
where the time goes in v3:
time: 65.5 us; the launch traced here: 65.4 us
  Pallas kernels  64 us (98%)
  other arithmetic  0.77 us (1%)
    pallas_call x1, Pallas kernels, per_device(): pl.pallas_call(functools.partial(kernel, nx, ny, nz), out_shape=(pltpu.VM...  64 us

profile of v3, /device:TPU:1, one launch (start us, length us, event | category | flops | bytes accessed | tf_op | source)
XLA Modules:
  0.0 65.4 jit_solution(11097310910002452705)
XLA Ops:
  0.6 64.0 %shard_map.86 = (f32[8,8,512]{2,1,0:T(8,128)S(1)}, f32[8,8,512]{2,1,0:T(8,128)S(1)}, f32[8,8,512]{2,1,0:T(8,128)S(1)}, f32[8,8,512]{2,1,0:T(8,128)S(1)}, f32[8,8...) custom-call(f32[8,8,512]{2,1,0:T(8,128)} %src_hbm.1, ...), custom_call_target="tpu_custom_call" | custom-call | tf_op jit(solution)/shard_map/pallas_call | solution.py:573
  64.6 0.8 %multiply_subtract_fusion = (f32[8,8,512]{2,1,0:T(8,128)}, f32[8,8,512]{2,1,0:T(8,128)}) fusion(f32[8,8,512]{2,1,0:T(8,128)S(1)} %get-tuple-element.16, f32[8,8,512]{2,1,0:T(8,128)S(1)} %get-tuple-element.17, f32[8,512]{1,0:T(8,128)S(1)} %get-tuple-element.13, f32[8,512]{1,0:T(8,128)S(1)} %get-tuple-element.11, f32[8,8,512]{2,1,0:T(8,128)S(1)} %get-tuple-element.14, ...), kind=kLoop, calls=%fused_computation | loop fusion | flops 327680 | bytes 1081344 | tf_op jit(solution)/shard_map/sub | solution.py:629

commit v4 on v3

--- a/solution.py
+++ b/solution.py
@@ -79,7 +79,7 @@
     nx, ny, nz,
     src_hbm, cond_hbm, flags_hbm, class_hbm, table_hbm, mats_hbm, planes_hbm,
     x_out, pp_out, r_out, pa_out, ra_out, pa2_out, al_out, om_out,
-    src, cond, w2, wk, wkt, flags, classes, table, mats, planes, mass, im,
+    src, rows, cond, w2, wk, wkt, flags, classes, table, mats, planes, mass, im,
     loc, vec, tmp, fx, fy, ywk, xr, yr, cr, ysend,
     parts, msg1, msg2, buf1, buf2,
     in_sem, send_x, send_y, send_c, recv_x, recv_y, recv_c,
@@ -98,8 +98,12 @@
         pltpu.make_async_copy(a, b, in_sem.at[i])
         for i, (a, b) in enumerate(
             [
-                (src_hbm, src),
+                (src_hbm.at[:, 0, :], rows.at[0]),
+                (src_hbm.at[:, 7, :], rows.at[1]),
+                (src_hbm.at[0], src.at[0]),
+                (src_hbm.at[7], src.at[7]),
                 (planes_hbm, planes),
+                (src_hbm.at[pl.ds(1, 6)], src.at[pl.ds(1, 6)]),
                 (cond_hbm, cond),
                 (mats_hbm, mats),
                 (flags_hbm, flags),
@@ -108,7 +112,7 @@
             ]
         )
     ]
-    for c in loads[:2]:
+    for c in loads[:6]:
         c.start()
 
     barrier = pltpu.get_barrier_semaphore()
@@ -118,7 +122,7 @@
     peers += [(gx, at_y(k)) for k in order_y] + [(at_x(k), gy) for k in order_x]
     for peer in peers:
         pl.semaphore_signal(barrier, inc=1, device_id=peer, device_id_type=MESH)
-    for c in loads[2:]:
+    for c in loads[6:]:
         c.start()
 
     lane = lax.broadcasted_iota(jnp.int32, (8, nz), 1)
@@ -154,7 +158,7 @@
     def across(y):
         return pl.ds(y, 8, stride=8)
 
-    for c in loads[:2]:
+    for c in loads[:5]:
         c.wait()
     w_yz = planes[0]
     inv_z = planes[1]
@@ -198,17 +202,20 @@
                 add = jnp.where(has, add, tile0)
                 vec.at[dst, t][across(7 * i), :] = vec.at[dst, t][across(7 * i), :] + add
 
-    for x in range(8):
-        put(loc.at[0], x, zfold(float(gll_weights[x]) * w_yz * src[x]))
-
+    end = float(gll_weights[0])
     for i in (0, 1):
-        for t in range(nt):
-            ysend[0, i, t] = loc.at[0, t][across(7 * i), :]
+        face = zfold(end * w_yz * rows[i])
+        for t, c in enumerate(chunks):
+            ysend[0, i, t] = face[:, c]
+        put(loc.at[0], 7 * i, zfold(end * w_yz * src[7 * i]))
     pl.semaphore_wait(barrier, len(peers))
     y_start(0)
     x_start(0)
-
-    for c in loads[2:]:
+    loads[5].wait()
+    for x in range(1, 7):
+        put(loc.at[0], x, zfold(float(gll_weights[x]) * w_yz * src[x]))
+
+    for c in loads[6:]:
         c.wait()
     bits = flags[...]
     kinds = classes[...]
@@ -577,6 +584,7 @@
             out_specs=(pl.BlockSpec(memory_space=pltpu.VMEM),) * 8,
             scratch_shapes=[
                 vm(field, f32),
+                vm((2, 8, nz), f32),
                 vm(field, f32),
                 vm(field, f32),
                 vm(flat, f32),
@@ -603,7 +611,7 @@
                 vm((SUMS, 1, 128), f32),
                 vm((SUMS, nx, 1, 128), f32),
                 vm((SUMS, ny, 1, 128), f32),
-                dma((7,)),
+                dma((11,)),
                 dma,
                 dma,
                 dma,

time: 65.5 us -> 65.6 us (level)
  no operation moved by 1% of the time
where the time goes in v4:
time: 65.6 us; the launch traced here: 65.4 us
  Pallas kernels  64 us (98%)
  other arithmetic  0.77 us (1%)
    pallas_call x1, Pallas kernels, per_device(): pl.pallas_call(functools.partial(kernel, nx, ny, nz), out_shape=(pltpu.VM...  64 us

profile of v4, /device:TPU:1, one launch (start us, length us, event | category | flops | bytes accessed | tf_op | source)
XLA Modules:
  0.0 65.4 jit_solution(10607230312839531635)
XLA Ops:
  0.6 64.0 %shard_map.86 = (f32[8,8,512]{2,1,0:T(8,128)S(1)}, f32[8,8,512]{2,1,0:T(8,128)S(1)}, f32[8,8,512]{2,1,0:T(8,128)S(1)}, f32[8,8,512]{2,1,0:T(8,128)S(1)}, f32[8,8...) custom-call(f32[8,8,512]{2,1,0:T(8,128)} %src_hbm.1, ...), custom_call_target="tpu_custom_call" | custom-call | tf_op jit(solution)/shard_map/pallas_call | solution.py:580
  64.7 0.8 %multiply_subtract_fusion = (f32[8,8,512]{2,1,0:T(8,128)}, f32[8,8,512]{2,1,0:T(8,128)}) fusion(f32[8,8,512]{2,1,0:T(8,128)S(1)} %get-tuple-element.16, f32[8,8,512]{2,1,0:T(8,128)S(1)} %get-tuple-element.17, f32[8,512]{1,0:T(8,128)S(1)} %get-tuple-element.13, f32[8,512]{1,0:T(8,128)S(1)} %get-tuple-element.11, f32[8,8,512]{2,1,0:T(8,128)S(1)} %get-tuple-element.14, ...), kind=kLoop, calls=%fused_computation | loop fusion | flops 327680 | bytes 1081344 | tf_op jit(solution)/shard_map/sub | solution.py:637

commit v5 on v4

--- a/solution.py
+++ b/solution.py
@@ -80,7 +80,7 @@
     src_hbm, cond_hbm, flags_hbm, class_hbm, table_hbm, mats_hbm, planes_hbm,
     x_out, pp_out, r_out, pa_out, ra_out, pa2_out, al_out, om_out,
     src, rows, cond, w2, wk, wkt, flags, classes, table, mats, planes, mass, im,
-    loc, vec, tmp, fx, fy, ywk, xr, yr, cr, ysend,
+    loc, vec, tmp, fx, fy, ywk, ymass, xr, yr, cr, ysend,
     parts, msg1, msg2, buf1, buf2,
     in_sem, send_x, send_y, send_c, recv_x, recv_y, recv_c,
     send_1, send_2, recv_1, recv_2,
@@ -263,6 +263,7 @@
             wkt[t, at(y), :] = wk.at[t][across(y), :]
         for i in (0, 1):
             ywk[pl.ds(8 * (i * nt + t), 8), :] = wk.at[t][across(7 * i), :]
+            ymass[pl.ds(8 * (i * nt + t), 8), :] = mass.at[t][across(7 * i), :]
 
     bf = jnp.bfloat16
 
@@ -298,12 +299,13 @@
             flux = [wk[t, at(x), :] * grad[x] - w2[x, :, chunks[t]] * v[x] for x in range(8)]
             back = along_planes(flux, D.T)
             for x in range(8):
-                fx[t, at(x), :] = mass[t, at(x), :] * v[x] + back[x]
+                fx[t, at(x), :] = back[x]
         for i in (0, 1):
             face = [
                 fx.at[t][across(7 * i), :]
                 + face_y[i][t]
                 + face_z[8 * (i * nt + t) : 8 * (i * nt + t) + 8]
+                + ymass[pl.ds(8 * (i * nt + t), 8), :] * vec.at[s, t][across(7 * i), :]
                 for t in range(nt)
             ]
             face = zfold(jnp.concatenate(face, axis=1))
@@ -322,7 +324,8 @@
             side = jnp.concatenate(
                 [back_z[64 * t + 8 * x : 64 * t + 8 * x + 8] for t in range(nt)], axis=1
             )
-            put(loc.at[k], x, zfold(get(tmp, x) + get(fx, x) + side))
+            local = get(mass, x) * get(vec.at[s], x) + get(fx, x)
+            put(loc.at[k], x, zfold(get(tmp, x) + local + side))
         x_start(k)
 
     parts[...] = jnp.zeros(parts.shape, f32)
@@ -398,13 +401,13 @@
     put_dot(0, 1, weighted(planes_of(B)), v1)
     put_dot(0, 2, weighted(v1), v1)
     halo_finish(2, V2)
-    apply_edges(V2, 3)
     v2 = planes_of(V2)
     v2w = weighted(v2)
     put_dot(0, 3, v2w, planes_of(B))
     put_dot(0, 4, v2w, planes_of(V1))
     put_dot(0, 5, v2w, v2)
     sum_start(0)
+    apply_edges(V2, 3)
     apply_rest(V2, 3)
     sum_middle(0)
     halo_finish(3, V3)
@@ -602,6 +605,7 @@
                 vm(flat, f32),
                 vm(flat, f32),
                 vm((16 * nt, 128), f32),
+                vm((16 * nt, 128), f32),
                 vm((ROUNDS, 2, nt, 8, 128), f32),
                 vm((ROUNDS, 2, nt, 8, 128), f32),
                 vm((ROUNDS, 2, nt, 8, 128), f32),

time: 65.6 us -> 65.6 us (level)
  no operation moved by 1% of the time
where the time goes in v5:
time: 65.6 us; the launch traced here: 65.5 us
  Pallas kernels  64.1 us (98%)
  other arithmetic  0.77 us (1%)
    pallas_call x1, Pallas kernels, per_device(): pl.pallas_call(functools.partial(kernel, nx, ny, nz), out_shape=(pltpu.VM...  64.1 us

profile of v5, /device:TPU:1, one launch (start us, length us, event | category | flops | bytes accessed | tf_op | source)
XLA Modules:
  0.0 65.5 jit_solution(2399358661023946057)
XLA Ops:
  0.6 64.1 %shard_map.86 = (f32[8,8,512]{2,1,0:T(8,128)S(1)}, f32[8,8,512]{2,1,0:T(8,128)S(1)}, f32[8,8,512]{2,1,0:T(8,128)S(1)}, f32[8,8,512]{2,1,0:T(8,128)S(1)}, f32[8,8...) custom-call(f32[8,8,512]{2,1,0:T(8,128)} %src_hbm.1, ...), custom_call_target="tpu_custom_call" | custom-call | tf_op jit(solution)/shard_map/pallas_call | solution.py:583
  64.7 0.8 %multiply_subtract_fusion = (f32[8,8,512]{2,1,0:T(8,128)}, f32[8,8,512]{2,1,0:T(8,128)}) fusion(f32[8,8,512]{2,1,0:T(8,128)S(1)} %get-tuple-element.16, f32[8,8,512]{2,1,0:T(8,128)S(1)} %get-tuple-element.17, f32[8,512]{1,0:T(8,128)S(1)} %get-tuple-element.13, f32[8,512]{1,0:T(8,128)S(1)} %get-tuple-element.11, f32[8,8,512]{2,1,0:T(8,128)S(1)} %get-tuple-element.14, ...), kind=kLoop, calls=%fused_computation | loop fusion | flops 327680 | bytes 1081344 | tf_op jit(solution)/shard_map/sub | solution.py:641
